TPU v7x, 256 devices: a whole 4x4x8 slice. The times are simulated.
256 devices in a mesh: wide: 32 (over y, x, core), narrow: 8 (over z).
Axes of the slice: x: 4, y: 4, z: 8, core: 2. Of those that a mesh axis runs over, the one named last changes fastest.
Arguments:
- constraint_rows: bfloat16 [512, 256, 1024], P(None, ('wide', 'narrow')), may hold values from -1 to 1
- metric: bfloat16 [1024, 1024], replicated, may hold values from -8 to 8, as said below
Outputs:
- factored: float32 [512, 256, 8, 128], P(None, 'wide', 'narrow')
Inputs may be any that keep to these rules, and one draw needn't show every extreme that they name: `metric`: symmetric and positive definite.
All inputs are finite; a program needn't handle non-finite values.
Results may differ from a plain program's by a relative error of at most 0.0052.
Values may be sent and summed in bfloat16 or wider, within the bound.
No kernel may reach another device: no remote copies, remote signals or barrier semaphores. Data moves between devices by JAX's collectives and lax.ppermute only.
A program may use at most 64 MiB of HBM per device.

v0:
```python
import jax
import jax.numpy as jnp
from jax import lax
from jax.sharding import PartitionSpec as P

P_SIZE = 1024
PB = 256
NPANEL = 2


def left_solve(factor_low, right_side):
    return jax.scipy.linalg.solve_triangular(factor_low, right_side, lower=True)


def strip_major(schur_slab, strips):
    row_count = schur_slab.shape[0]
    strip_len = schur_slab.shape[1] // strips
    reordered = schur_slab.reshape(row_count, strip_len, strips).transpose(0, 2, 1)
    return reordered.reshape(row_count, 1, strips, strip_len)


def local(constraint_rows, metric):
    groups = lax.axis_size(("wide", "narrow"))
    strips = lax.axis_size("narrow")
    row_count = constraint_rows.shape[0]
    panel_depth = P_SIZE // groups
    block_rows = PB // groups
    flat_rows = constraint_rows[:, 0, :]
    projected = jnp.dot(flat_rows, metric, preferred_element_type=jnp.float32).astype(jnp.bfloat16)
    gram_cols = jnp.einsum(
        "rn,kmn->rkm",
        projected,
        lax.all_gather(constraint_rows[:panel_depth], ("wide", "narrow"), axis=1, tiled=True),
        preferred_element_type=jnp.float32,
    )
    schur_slab = (gram_cols * gram_cols).reshape(row_count, P_SIZE)
    grid_block = lax.all_to_all(
        strip_major(schur_slab, strips), "narrow", split_axis=2, concat_axis=1, tiled=True
    )
    strip_len = P_SIZE // strips
    grid_rows = row_count * strips
    narrow_panel = PB // strips
    own_strip = lax.axis_index("narrow")
    flat_block = grid_block.reshape(grid_rows, strip_len)
    for panel_number in range(NPANEL):
        col_begin = panel_number * PB
        row_begin = col_begin // groups
        strip_begin = col_begin // strips
        strip_end = strip_begin + narrow_panel
        own_rows = flat_block.reshape(row_count, strips, strip_len)[
            row_begin : row_begin + block_rows, :, strip_begin:
        ]
        shared = lax.all_gather(own_rows, "wide", axis=1, tiled=True)
        shared = shared.reshape(PB, strip_len - strip_begin)
        diag_strip, row_strip = (
            lax.all_gather(shared[:, :narrow_panel], "narrow", axis=1, tiled=True),
            lax.all_gather(flat_block[:, strip_begin:strip_end], "narrow", axis=1, tiled=True),
        )
        diag_block = diag_strip.reshape(PB, strips, narrow_panel).transpose(0, 2, 1).reshape(PB, PB)
        panel_cols = (
            row_strip.reshape(grid_rows, strips, narrow_panel)
            .transpose(0, 2, 1)
            .reshape(grid_rows, PB)
        )
        factor_low = jnp.linalg.cholesky(diag_block)
        upper_part = left_solve(factor_low, shared[:, narrow_panel:])
        column = left_solve(factor_low, panel_cols.T).T
        trailing = flat_block[:, strip_end:] - jnp.dot(
            column, upper_part, precision=lax.Precision.HIGHEST
        )
        own_cols = lax.dynamic_index_in_dim(
            column.reshape(grid_rows, narrow_panel, strips), own_strip, 2, keepdims=False
        )
        flat_block = jnp.concatenate([flat_block[:, :strip_begin], own_cols, trailing], axis=1)
    return flat_block.reshape(row_count, strips, 1, strip_len)


def solution(mesh):
    placed = (P(None, ("wide", "narrow"), None), P())
    return jax.shard_map(
        local,
        mesh=mesh,
        in_specs=placed,
        out_specs=P(None, "wide", "narrow", None),
        check_vma=False,
    )
```

profile of v0, /device:TPU:1, one launch (start us, length us, event | category | flops | bytes accessed | tf_op | source)
XLA Modules:
  0.0 463.1 jit_solution(18273028846116087548)
XLA Ops:
  8.1 111.3 %all-gather.6.cloned.1.call-done = bf16[4,256,1024]{2,0,1:T(4,128)(2,1)} async-done(((bf16[4,1,1024]{2,0,1:T(4,128)(2,1)}), bf16[4,256,1024]{2,0,1:T(4,128)(2,1)}) %all-gather.6.cloned.1.call-update) | async-done | bytes 2097168 | tf_op jit(solution)/shard_map/all_gather | solution.py:33
  119.4 5.7 %fusion.8 = f32[512,4,256]{0,2,1:T(8,128)} fusion(bf16[4,256,1024]{2,0,1:T(4,128)(2,1)} %all-gather.6.cloned.1.call-done, bf16[1024,1024]{1,0:T(8,128)(2,1)S(1)} %copy-done, bf16[512,1,1024]{2,0,1:T(8,128)(2,1)} %param.5), kind=kOutput, calls=%fused_computation.22 | convolution fusion | flops 2148532224 | bytes 7340032 | tf_op jit(solution)/shard_map/rn,kmn->rkm/dot_general | solution.py:30
  127.1 55.5 %all_to_all.4 = f32[512,1,8,128]{3,1,0,2:T(1,128)S(1)} all-to-all(f32[512,1,8,128]{3,1,0,2:T(1,128)S(1)} %bitcast.153), channel_id=1, replica_groups=mesh['wide'=32,'narrow'=8] {'narrow'}, dimensions={2} | all-to-all | bytes 4194304 | tf_op jit(solution)/shard_map/all_to_all | solution.py:37
  187.3 25.5 %all-gather = f32[1,1,256,128]{3,2,1,0:T(8,128)S(1)} all-gather(f32[1,1,8,128]{3,2,1,0:T(8,128)S(1)} %bitcast.150), channel_id=2, replica_groups=mesh['wide'=32,'narrow'=8] {'wide'}, dimensions={2}, use_global_device_ids=true | all-gather | bytes 135168 | tf_op jit(solution)/shard_map/all_gather | solution.py:53
  213.0 23.1 %all_gather.23 = f32[256,256]{0,1:T(8,128)S(1)} all-gather(f32[256,32]{0,1:T(8,128)S(1)} %copy.64), channel_id=1, replica_groups=mesh['wide'=32,'narrow'=8] {'narrow'}, dimensions={1}, use_global_device_ids=true | all-gather | bytes 294912 | tf_op jit(solution)/shard_map/all_gather | solution.py:56
  236.7 11.7 %cholesky.130 = f32[128,128]{1,0:T(8,128)S(1)} custom-call(f32[128,128]{1,0:T(8,128)S(1)} %cholesky.194), custom_call_target="Cholesky" | custom-call | tf_op jit(solution)/shard_map/jit(cholesky)/cholesky | solution.py:65
  248.4 9.8 %custom-call.23 = f32[1,128,128]{1,2,0:T(8,128)S(1)} custom-call(f32[1,128,128]{2,1,0:T(8,128)S(1)} %get-tuple-element.66), custom_call_target="InvertDiagBlocksLowerTriangular" | custom-call | tf_op jit(solution)/shard_map/jit(cholesky)/cholesky | solution.py:65
  258.7 11.7 %cholesky.147 = f32[128,128]{1,0:T(8,128)S(1)} custom-call(f32[128,128]{1,0:T(8,128)S(1)} %convolution_subtract_fusion.5), custom_call_target="Cholesky" | custom-call | tf_op jit(solution)/shard_map/jit(cholesky)/cholesky | solution.py:65
  272.5 3.9 while.6
  276.4 19.7 %custom-call.24 = f32[2,128,128]{1,2,0:T(8,128)S(1)} custom-call(f32[2,128,128]{2,1,0:T(8,128)S(1)} %get-tuple-element.37), custom_call_target="InvertDiagBlocksLowerTriangular" | custom-call | tf_op jit(solution)/shard_map/jit(_solve_triangular)/triangular_solve | solution.py:12
  296.1 2.1 copy.83
  299.1 4.6 copy.99
  309.6 2.7 convolution_subtract_fusion.2
  315.3 27.5 %all-gather.1 = f32[256,96]{1,0:T(8,128)S(1)} all-gather(f32[8,96]{1,0:T(8,128)S(1)} %copy.73), channel_id=3, replica_groups=mesh['wide'=32,'narrow'=8] {'wide'}, dimensions={0}, use_global_device_ids=true | all-gather | bytes 101376 | tf_op jit(solution)/shard_map/all_gather | solution.py:53
  343.1 23.0 %all_gather.26 = f32[256,256]{0,1:T(8,128)S(1)} all-gather(f32[256,32]{0,1:T(8,128)S(1)} %copy.85), channel_id=1, replica_groups=mesh['wide'=32,'narrow'=8] {'narrow'}, dimensions={1}, use_global_device_ids=true | all-gather | bytes 294912 | tf_op jit(solution)/shard_map/all_gather | solution.py:56
  366.6 11.7 %cholesky.164 = f32[128,128]{1,0:T(8,128)S(1)} custom-call(f32[128,128]{1,0:T(8,128)S(1)} %cholesky.197), custom_call_target="Cholesky" | custom-call | tf_op jit(solution)/shard_map/jit(cholesky)/cholesky | solution.py:65
  378.3 9.8 %custom-call.25 = f32[1,128,128]{1,2,0:T(8,128)S(1)} custom-call(f32[1,128,128]{2,1,0:T(8,128)S(1)} %get-tuple-element.62), custom_call_target="InvertDiagBlocksLowerTriangular" | custom-call | tf_op jit(solution)/shard_map/jit(cholesky)/cholesky | solution.py:65
  388.6 11.7 %cholesky.181 = f32[128,128]{1,0:T(8,128)S(1)} custom-call(f32[128,128]{1,0:T(8,128)S(1)} %convolution_subtract_fusion.4), custom_call_target="Cholesky" | custom-call | tf_op jit(solution)/shard_map/jit(cholesky)/cholesky | solution.py:65
  403.0 3.9 while.7
  406.8 19.7 %custom-call.26 = f32[2,128,128]{1,2,0:T(8,128)S(1)} custom-call(f32[2,128,128]{2,1,0:T(8,128)S(1)} %get-tuple-element.38), custom_call_target="InvertDiagBlocksLowerTriangular" | custom-call | tf_op jit(solution)/shard_map/jit(_solve_triangular)/triangular_solve | solution.py:12
  426.5 2.0 fusion.1
  431.8 4.6 copy.98
  443.7 2.9 convolution_subtract_fusion.3
  450.8 5.5 %pad_maximum_fusion.4 = f32[512,8,1,128]{3,1,0,2:T(8,128)} fusion(f32[512,8,1,64]{3,1,0,2:T(8,128)} %bitcast.154, f32[512,8,1,32]{3,1,0,2:T(8,128)} %bitcast.152, f32[512,8,1,32]{3,1,0,2:T(8,128)} %bitcast.151), kind=kLoop, calls=%fused_computation.18 | loop fusion | flops 1048576 | bytes 4194304 | tf_op jit(solution)/shard_map/concatenate | solution.py:74
  (97 shorter events, 44.8 us)
Async XLA Ops:
  6.5 112.9 %copy-start = (bf16[1024,1024]{1,0:T(8,128)(2,1)S(1)}, bf16[1024,1024]{1,0:T(8,128)(2,1)}, u32[]{:S(2)}) copy-start(bf16[1024,1024]{1,0:T(8,128)(2,1)} %param.6) | copy-start | bytes 6291460
  6.5 112.8 %all-gather.6.cloned.1.call-start = ((), (), s32[]{:S(2)}) async-start(), calls=%async_computation.1 | async-start | bytes 2105344 | tf_op jit(solution)/shard_map/all_gather | solution.py:33
  8.0 291.0 %all-gather.8.cloned.1.call-start = ((), (), s32[]{:S(2)}) async-start(), calls=%async_computation.2 | async-start | bytes 4718592 | tf_op jit(solution)/shard_map/all_gather | solution.py:57
  182.6 1.3 copy-start.3
  185.3 246.5 %all-gather.10.cloned.1.call-start = ((), (), s32[]{:S(2)}) async-start(), calls=%async_computation.3 | async-start | bytes 4718592 | tf_op jit(solution)/shard_map/all_gather | solution.py:57
  185.4 1.9 slice-start
  236.3 59.8 %copy-start.4 = (f32[4096,96]{1,0:T(8,128)S(1)}, f32[4096,96]{1,0:T(8,128)}, u32[]{:S(2)}) copy-start(f32[4096,96]{1,0:T(8,128)} %slice.153) | copy-start | bytes 4718596
  307.6 2.0 copy-start.7
  309.6 2.8 copy-start.2
  312.3 1.1 copy-start.5
  442.3 1.4 copy-start.6
  450.8 5.5 %copy-start.1 = (bf16[1024,1024]{1,0:T(8,128)(2,1)S(1)}, bf16[1024,1024]{1,0:T(8,128)(2,1)}, u32[]{:S(2)}) copy-start(bf16[1024,1024]{1,0:T(8,128)(2,1)} %param.6) | copy-start | bytes 6291460
Sparse Core Ops, SparseCore 0:
  11.1 108.2 all-gather.5
  185.4 53.2 all-gather.7
  314.5 54.9 all-gather.9
where the time goes:
time: 469 us; the launch traced here: 463 us
  blocking collectives  155 us (33%)
  other arithmetic  116 us (25%)
  waiting for transfers between devices  111 us (24%)
  local copies, waits for them, and re-layouts  38.9 us (8%)
  matrix products  25.5 us (5%)
  between operations  16.2 us (3%)
    all_gather x1, waiting for transfers between devices, local(): lax.all_gather(constraint_rows[:panel_depth], ('wide', 'narrow'), axis=1,...  111 us
    another operation x13, other arithmetic, local(): factor_low = jnp.linalg.cholesky(diag_block)  68.6 us
    all_to_all x1, blocking collectives, local(): lax.all_to_all(strip_major(schur_slab, strips), 'narrow', split_axis=2, c...  55.5 us
    all_gather x2, blocking collectives, local(): shared = lax.all_gather(own_rows, 'wide', axis=1, tiled=True)  53 us
    all_gather x2, blocking collectives, local(): lax.all_gather(shared[:, :narrow_panel], 'narrow', axis=1, tiled=True)  46.1 us
    another operation x5, other arithmetic, left_solve(): return jax.scipy.linalg.solve_triangular(factor_low, right_side, lower=True)  39.4 us
    another operation x12, matrix products, left_solve(): return jax.scipy.linalg.solve_triangular(factor_low, right_side, lower=True)  13.2 us
  transfers between devices with their start and end apart: 3, of which 1 were waited for; matrix products, arithmetic and copies ran while one was open for 28% of the time, Pallas kernels for 0%

commit v1 on v0

v1 whole, which is shorter than its diff:
```python
import functools

import jax
import jax.numpy as jnp
from jax import lax
from jax.experimental import pallas as pl
from jax.experimental.pallas import tpu as pltpu
from jax.sharding import PartitionSpec as P

PB = 256
F32 = jnp.float32
BF16 = jnp.bfloat16
HIGHEST = lax.Precision.HIGHEST
VMEM = pl.BlockSpec(memory_space=pltpu.VMEM)


def mm(a, b):
    return jnp.dot(a, b, preferred_element_type=F32)


def mm_nt(a, b):
    return lax.dot_general(a, b, (((1,), (1,)), ((), ())), preferred_element_type=F32)


def fmm(a, b):
    return jnp.dot(a, b, precision=HIGHEST, preferred_element_type=F32)


def fmm_nt(a, b):
    return lax.dot_general(
        a, b, (((1,), (1,)), ((), ())), precision=HIGHEST, preferred_element_type=F32
    )


def square(x):
    return x * x


def over_lanes(x, j):
    return jnp.broadcast_to(x[:, j : j + 1], x.shape)


def over_rows(x, m):
    return jnp.broadcast_to(x[m : m + 1, :], x.shape)


def inverse_factor(matrix, store):
    n = matrix.shape[1]
    tiles = [matrix[8 * i : 8 * i + 8, :] for i in range(n // 8)]
    row = lax.broadcasted_iota(jnp.int32, (8, n), 0)
    lane = lax.broadcasted_iota(jnp.int32, (8, n), 1)
    for b in range(n // 8):
        pivot = tiles[b]
        cols = [over_lanes(pivot, 8 * b + m) for m in range(8)]
        result = jnp.zeros((8, n), F32)
        for m in range(8):
            j = 8 * b + m
            d = over_rows(cols[m], m)
            r = 1.0 / d
            here = row == m
            mult = jnp.where(here, -r, cols[m] * r)
            prow = jnp.where(lane == j, 1.0, over_rows(pivot, m))
            result = jnp.where(here & (lane <= j), prow * lax.rsqrt(d), result)
            pivot = jnp.where(here | (lane == j), 0.0, pivot) - mult * prow
            for k in range(m + 1, 8):
                cols[k] = jnp.where(here, 0.0, cols[k]) - mult * over_rows(cols[k], m)
        store(b, result)
        if b + 1 < n // 8:
            rows = [over_rows(pivot, m) for m in range(8)]
            keep = (lane < 8 * b) | (lane >= 8 * b + 8)
            for i in range(b + 1, n // 8):
                t = [over_lanes(tiles[i], 8 * b + m) * rows[m] for m in range(8)]
                t = ((t[0] + t[1]) + (t[2] + t[3])) + ((t[4] + t[5]) + (t[6] + t[7]))
                tiles[i] = jnp.where(keep, tiles[i], 0.0) - t


def factor_block(block, out_ref, half=128):
    def writer(base):
        def store(i, tile):
            out_ref[base + 8 * i : base + 8 * i + 8, base : base + half] = tile

        return store

    out_ref[:half, half:] = jnp.zeros((half, half), F32)
    inverse_factor(block[:half, :half], writer(0))
    top = out_ref[:half, :half]
    lower = fmm_nt(block[half:, :half], top)
    inverse_factor(block[half:, half:] - fmm_nt(lower, lower), writer(half))
    out_ref[half:, :half] = -fmm(out_ref[half:, half:], fmm(lower, top))


def own_kernel(rows_ref, metric_ref, proj_ref, spread_ref, spread_t_ref):
    proj_ref[...] = mm(rows_ref[...], metric_ref[...]).astype(BF16)
    for ref, cols in ((spread_ref, 256), (spread_t_ref, 512)):
        per = cols // 8
        r = lax.broadcasted_iota(jnp.int32, (1024, 1024), 0)
        c = lax.broadcasted_iota(jnp.int32, (1024, 1024), 1)
        dst, lane = c // 128, c % 128
        want = (lane // per) * cols + (lane % per) * 8 + dst
        ref[...] = jnp.where(r == want, 1.0, 0.0).astype(BF16)


def first_kernel(panel_ref, metric_ref, proj_ref, inv_ref):
    panel = panel_ref[...]
    proj = mm(panel, metric_ref[...]).astype(BF16)
    proj_ref[...] = proj
    diag = square(mm_nt(proj, panel))
    factor_block(0.5 * (diag + diag.T), inv_ref)


def packed(values, groups, spread):
    size = values.shape[0] // groups
    side = jnp.concatenate([values[g * size : (g + 1) * size] for g in range(groups)], axis=1)
    return mm(side.astype(BF16), spread).astype(BF16)


def middle_kernel(
    own_proj_ref, p0_ref, inv_ref, panel_ref, later_ref, metric_ref, spread_ref,
    schur_ref, upper_ref, low_ref, col_ref, send_ref,
):
    v0, v1, inv = panel_ref[...], later_ref[:PB], inv_ref[...]
    col = fmm_nt(square(mm_nt(own_proj_ref[...], v0)), inv)
    col_ref[...] = col
    strips = packed(col, 4, spread_ref[...])
    for s in range(8):
        send_ref[s] = strips[:, 128 * s : 128 * s + 128]
    upper = fmm(inv, square(mm_nt(p0_ref[...], later_ref[...])))
    upper_ref[...] = upper
    p1 = mm(v1, metric_ref[...]).astype(BF16)
    low = fmm_nt(square(mm_nt(p1, v0)), inv)
    low_ref[...] = low
    slab = square(mm_nt(p1, later_ref[...])) - fmm(low, upper)
    schur_ref[...] = slab


def second_kernel(schur_ref, inv_ref):
    diag = schur_ref[:, :PB]
    factor_block(0.5 * (diag + diag.T), inv_ref)


def last_kernel(
    own_proj_ref, later_ref, col_ref, upper_ref, schur_ref, inv_ref, spread_ref, spread_t_ref,
    send_ref,
):
    inv = inv_ref[...]
    slab = square(mm_nt(own_proj_ref[...], later_ref[...])) - fmm(col_ref[...], upper_ref[...])
    col = fmm_nt(slab[:, :PB], inv)
    strips = packed(col, 4, spread_ref[...])
    for s in range(8):
        send_ref[s, :128] = strips[:, 128 * s : 128 * s + 128]
    upper = fmm(inv, schur_ref[:, PB:])
    trail = packed(slab[:, PB:] - fmm(col, upper), 2, spread_t_ref[...])
    for s in range(8):
        send_ref[s, 128:] = trail[:, 128 * s : 128 * s + 128]


def join_kernel(first_ref, rest_ref, out_ref):
    lane = lax.broadcasted_iota(jnp.int32, (128, 128), 1)
    for s in range(8):
        a = first_ref[s].astype(F32)
        b = rest_ref[s, :128].astype(F32)
        t = [rest_ref[s, 128:256].astype(F32), rest_ref[s, 256:].astype(F32)]
        for g in range(4):
            x = pltpu.roll(a, (-32 * g) % 128, 1)
            y = pltpu.roll(b, (32 - 32 * g) % 128, 1)
            z = pltpu.roll(t[g % 2], (64 - 64 * (g // 2)) % 128, 1)
            out_ref[pl.ds(1024 * g + s, 128, stride=8), :] = jnp.where(
                lane < 32, x, jnp.where(lane < 64, y, z)
            )


def call(kernel, outs, flops, name):
    shapes = [jax.ShapeDtypeStruct(s, t) for s, t in outs]
    single = len(shapes) == 1
    return pl.pallas_call(
        kernel,
        out_shape=shapes[0] if single else shapes,
        name=name,
        compiler_params=pltpu.CompilerParams(vmem_limit_bytes=56 << 20),
        cost_estimate=pl.CostEstimate(flops=flops, bytes_accessed=4 << 20, transcendentals=0),
    )


def spread_to(value, count, axis, groups=None):
    wide = jnp.broadcast_to(value[None], (count,) + value.shape)
    return lax.all_to_all(wide, axis, 0, 0, tiled=True, axis_index_groups=groups)


def local(constraint_rows, metric):
    cores = 2
    plane = lax.axis_size("wide") // cores
    narrow = lax.axis_size("narrow")
    same_core = [[cores * i + c for i in range(plane)] for c in range(cores)]
    swap = [(i, i ^ 1) for i in range(plane * cores)]
    core = lax.axis_index("wide") % cores
    rows = constraint_rows[:, 0, :]
    row_count, n = rows.shape

    def gathered(block):
        mine = spread_to(block, plane, "wide", same_core)
        other = lax.ppermute(mine, "wide", swap)
        return jnp.where(
            core == 0, jnp.stack([mine, other], 1), jnp.stack([other, mine], 1)
        )

    column = spread_to(rows[:4], narrow, "narrow")
    own_proj, spread, spread_t = call(
        own_kernel, [((row_count, n), BF16), ((1024, 1024), BF16), ((1024, 1024), BF16)], 4 << 30, "own"
    )(rows, metric)
    panel = gathered(column[:, 0]).reshape(PB, n)
    later = gathered(column[:, 1:].transpose(1, 0, 2))
    later = later.transpose(2, 0, 1, 3, 4).reshape(3 * PB, n)
    p0, inv0 = call(first_kernel, [((PB, n), BF16), ((PB, PB), F32)], 16 << 30, "first")(panel, metric)
    schur, upper, low, col, send0 = call(
        middle_kernel,
        [((PB, 3 * PB), F32), ((PB, 3 * PB), F32), ((PB, PB), F32), ((row_count, PB), F32), ((8, 128, 128), BF16)],
        4 << 30, "middle",
    )(own_proj, p0, inv0, panel, later, metric, spread)
    got0 = lax.all_to_all(send0, "narrow", 0, 0, tiled=True)
    inv1 = call(second_kernel, [((PB, PB), F32)], 16 << 30, "second")(schur)
    send1 = call(last_kernel, [((8, 384, 128), BF16)], 4 << 30, "last")(
        own_proj, later, col, upper, schur, inv1, spread, spread_t
    )
    got1 = lax.all_to_all(send1, "narrow", 0, 0, tiled=True)
    out = call(join_kernel, [((row_count * 8, 128), F32)], 1 << 30, "join")(got0, got1)
    return out.reshape(row_count, 8, 1, 128)


def solution(mesh):
    placed = (P(None, ("wide", "narrow"), None), P())
    return jax.shard_map(
        local,
        mesh=mesh,
        in_specs=placed,
        out_specs=P(None, "wide", "narrow", None),
        check_vma=False,
    )
```

time: 469 us -> 136 us (0.29); the launches traced: 463 us -> 135 us
  other arithmetic: 116 us -> 1.12 us
  blocking collectives: 155 us -> 45.5 us
  waiting for transfers between devices: 111 us -> 7.62 us
  Pallas kernels: 0 us -> 55 us
  local copies, waits for them, and re-layouts: 38.9 us -> 3.88 us
  matrix products: 25.5 us -> 0 us
  starting transfers between devices: 0.09 us -> 22 us
  between operations: 16.2 us -> 0.08 us
    all_gather x3 -> x0, waiting for transfers between devices: 111 us -> none  [the longest x1 111 us: local(): lax.all_gather(constraint_rows[:panel_depth], ('wide', 'narrow'), axis=1,...]
    another operation x18 -> x0, other arithmetic: 108 us -> none  [the longest x13 68.6 us: local(): factor_low = jnp.linalg.cholesky(diag_block)]
    all_gather x4 -> x0, blocking collectives: 99.1 us -> none  [the longest x2 53 us: local(): shared = lax.all_gather(own_rows, 'wide', axis=1, tiled=True)]
    pallas_call x0 -> x6, Pallas kernels: none -> 55 us  [the longest x1 13.7 us: local(): call(first_kernel, [((PB, n), BF16), ((PB, PB), F32)], 16 << 30, 'first')]
    another operation x16 -> x0, matrix products: 14.2 us -> none  [the longest x12 13.2 us: left_solve(): return jax.scipy.linalg.solve_triangular(factor_low, right_side, lower=True)]
    all_to_all x0 -> x3, starting transfers between devices: none -> 14 us  [the longest x2 10.4 us: spread_to(): lax.all_to_all(wide, axis, 0, 0, tiled=True, axis_index_groups=groups)]
    dot_general x3 -> x0, matrix products: 11.3 us -> none  [the longest x1 5.7 us: local(): jnp.einsum('rn,kmn->rkm', projected, lax.all_gather(constraint_rows[:pane...]
    all_to_all x1 -> x2, blocking collectives: 55.5 us -> 45.5 us  [the longest x1 29.4 us: local(): got1 = lax.all_to_all(send1, 'narrow', 0, 0, tiled=True)]
  transfers between devices with their start and end apart: 3 -> 5, of which waited for: 1 -> 2; matrix products, arithmetic and copies ran while one was open for 28% -> 1% of each run, Pallas kernels for 0% -> 31%
where the time goes in v1:
time: 136 us; the launch traced here: 135 us
  Pallas kernels  55 us (40%)
  blocking collectives  45.5 us (33%)
  starting transfers between devices  22 us (16%)
  waiting for transfers between devices  7.62 us (6%)
  local copies, waits for them, and re-layouts  3.88 us (3%)
    all_to_all x1, blocking collectives, local(): got1 = lax.all_to_all(send1, 'narrow', 0, 0, tiled=True)  29.4 us
    all_to_all x1, blocking collectives, spread_to(): lax.all_to_all(wide, axis, 0, 0, tiled=True, axis_index_groups=groups)  16 us
    pallas_call x1, Pallas kernels, local(): call(first_kernel, [((PB, n), BF16), ((PB, PB), F32)], 16 << 30, 'first')  13.7 us
    pallas_call x1, Pallas kernels, local(): inv1 = call(second_kernel, [((PB, PB), F32)], 16 << 30, 'second')(schur)  12.2 us
    all_to_all x2, starting transfers between devices, spread_to(): lax.all_to_all(wide, axis, 0, 0, tiled=True, axis_index_groups=groups)  10.4 us
    pallas_call x1, Pallas kernels, local(): call(last_kernel, [((8, 384, 128), BF16)], 4 << 30, 'last')  10 us
    pallas_call x1, Pallas kernels, local(): call(middle_kernel, [((PB, 3 * PB), F32), ((PB, 3 * PB), F32), ((PB, PB),...  9.37 us
    ppermute x2, starting transfers between devices, gathered(): other = lax.ppermute(mine, 'wide', swap)  8 us
  transfers between devices with their start and end apart: 5, of which 2 were waited for; matrix products, arithmetic and copies ran while one was open for 1% of the time, Pallas kernels for 31%

profile of v1, /device:TPU:1, one launch (start us, length us, event | category | flops | bytes accessed | tf_op | source)
XLA Modules:
  0.0 135.2 jit_solution(11583899893648646610)
XLA Ops:
  0.0 0.7 slice_bitcast_fusion.1
  0.7 16.0 %all_to_all.25 = bf16[8,4,1024]{2,1,0:T(4,128)(2,1)S(1)} all-to-all(bf16[8,4,1024]{2,1,0:T(4,128)(2,1)S(1)} %broadcast_in_dim.22), channel_id=1, replica_groups=mesh['wide'=32,'narrow'=8] {'narrow'}, dimensions={0} | all-to-all | bytes 131072 | tf_op jit(solution)/shard_map/all_to_all | solution.py:186
  16.8 0.7 broadcast_in_dim.24
  17.6 6.8 %all-to-all-start.1 = ((bf16[16,8,1024]{2,1,0:T(8,128)(2,1)}), bf16[16,8,1024]{2,1,0:T(8,128)(2,1)S(1)}, u32[]{:S(2)}, u32[]{:S(2)}) async-start(bf16[16,8,1024]{2,1,0:T(8,128)(2,1)} %broadcast_in_dim.24), calls=%async_computation.1 | async-start | bytes 524288 | tf_op jit(solution)/shard_map/all_to_all | solution.py:186
  24.4 7.5 %all-to-all-done.1 = bf16[16,8,1024]{2,1,0:T(8,128)(2,1)S(1)} async-done(((bf16[16,8,1024]{2,1,0:T(8,128)(2,1)}), bf16[16,8,1024]{2,1,0:T(8,128)(2,1)S(1)}, u32[]{:S(2)}, u32[]{:S(2)}) %all-to-all-start.1) | async-done | bytes 262176 | tf_op jit(solution)/shard_map/all_to_all | solution.py:186
  31.9 1.0 broadcast_in_dim.25
  32.8 3.6 %all-to-all-start.2 = ((bf16[16,3,8,1024]{3,2,1,0:T(8,128)(2,1)}), bf16[16,3,8,1024]{3,2,1,0:T(8,128)(2,1)S(1)}, u32[]{:S(2)}, u32[]{:S(2)}) async-start(bf16[16,3,8,1024]{3,2,1,0:T(8,128)(2,1)} %broadcast_in_dim.25), calls=%async_computation.2 | async-start | bytes 1572864 | tf_op jit(solution)/shard_map/all_to_all | solution.py:186
  36.5 3.6 %collective-permute-start = (bf16[16,8,1024]{2,1,0:T(8,128)(2,1)S(1)}, bf16[16,8,1024]{2,1,0:T(8,128)(2,1)S(1)}, u32[]{:S(2)}, u32[]{:S(2)}) collective-permute-start(bf16[16,8,1024]{2,1,0:T(8,128)(2,1)S(1)} %all-to-all-done.1), channel_id=1, source_target_pairs={{0,8},{8,0},{16,24},{24,16},{32,40},{40,32},{48,56},{56,48},{64,72... | collective-permute-start | bytes 786440 | tf_op jit(solution)/shard_map/ppermute | solution.py:201
  40.1 6.4 %own.1 = (bf16[512,1024]{1,0:T(8,128)(2,1)}, bf16[1024,1024]{1,0:T(8,128)(2,1)}, bf16[1024,1024]{1,0:T(8,128)(2,1)}) custom-call(bf16[512,1024]{1,0:T(8,128)(2,1)} %bitcast.28, bf16[1024,1024]{1,0:T(8,128)(2,1)} %metric_ref.5), custom_call_target="tpu_custom_call" | custom-call | flops 4294967296 | bytes 4194304 | tf_op jit(solution)/shard_map/own/pallas_call | solution.py:207
  46.4 0.0 collective-permute-done
  46.5 0.9 maximum_select_fusion.1
  47.3 0.1 all-to-all-done.2
  47.5 4.4 %collective-permute-start.1 = (bf16[16,3,8,1024]{3,2,1,0:T(8,128)(2,1)S(1)}, bf16[16,3,8,1024]{3,2,1,0:T(8,128)(2,1)S(1)}, u32[]{:S(2)}, u32[]{:S(2)}) collective-permute-start(bf16[16,3,8,1024]{3,2,1,0:T(8,128)(2,1)S(1)} %all-to-all-done.2), channel_id=1, source_target_pairs={{0,8},{8,0},{16,24},{24,16},{32,40},{40,32},{48,56},{56,48},{64,72... | collective-permute-start | bytes 2359304 | tf_op jit(solution)/shard_map/ppermute | solution.py:201
  51.9 13.7 %first.1 = (bf16[256,1024]{1,0:T(8,128)(2,1)}, f32[256,256]{1,0:T(8,128)}) custom-call(bf16[256,1024]{1,0:T(8,128)(2,1)} %bitcast.24, bf16[1024,1024]{1,0:T(8,128)(2,1)} %metric_ref.5), custom_call_target="tpu_custom_call" | custom-call | flops 17179869184 | bytes 4194304 | tf_op jit(solution)/shard_map/first/pallas_call | solution.py:213
  65.6 0.0 collective-permute-done.1
  65.6 0.3 fusion
  65.9 1.3 copy.9
  67.2 9.4 %middle.1 = (f32[256,768]{1,0:T(8,128)}, f32[256,768]{1,0:T(8,128)}, f32[256,256]{1,0:T(8,128)}, f32[512,256]{1,0:T(8,128)}, bf16[8,128,128]{2,1,0:T(8,128)(2,1)}) custom-call(bf16[512,1024]{1,0:T(8,128)(2,1)} %get-tuple-element.14.own_proj_ref, bf16[256,1024]{1,0:T(8,128)(2,1)} %get-tuple-element.15.p0_ref, f32[256,256]{1,0:T(8,128)} %get-tuple-element.16.inv_ref, ...), custom_call_target="tpu_custom_call" | custom-call | flops 4294967296 | bytes 4194304 | tf_op jit(solution)/shard_map/middle/pallas_call | solution.py:214
  76.6 3.6 %all-to-all-start.3 = ((bf16[8,128,128]{2,1,0:T(8,128)(2,1)}), bf16[8,128,128]{2,1,0:T(8,128)(2,1)S(1)}, u32[]{:S(2)}, u32[]{:S(2)}) async-start(bf16[8,128,128]{2,1,0:T(8,128)(2,1)} %get-tuple-element.18), calls=%async_computation.3 | async-start | bytes 524288 | tf_op jit(solution)/shard_map/all_to_all | solution.py:219
  80.2 12.2 %second.1.inv_ref = f32[256,256]{1,0:T(8,128)} custom-call(f32[256,768]{1,0:T(8,128)} %get-tuple-element.21.schur_ref), custom_call_target="tpu_custom_call" | custom-call | flops 17179869184 | bytes 4194304 | tf_op jit(solution)/shard_map/second/pallas_call | solution.py:220
  92.4 10.0 %last.1 = bf16[8,384,128]{2,1,0:T(8,128)(2,1)} custom-call(bf16[512,1024]{1,0:T(8,128)(2,1)} %get-tuple-element.14.own_proj_ref, bf16[768,1024]{1,0:T(8,128)(2,1)} %bitcast.21, f32[512,256]{1,0:T(8,128)} %get-tuple-element.19.col_ref, f32[256,768]{1,0:T(8,128)} %get-tuple-element.20.upper_ref, f32[256,768]{1,0:T(8,128)} %get-tuple-element.21.schur_ref, ...), custom_call_target="tpu_custom_call" | custom-call | flops 4294967296 | bytes 4194304 | tf_op jit(solution)/shard_map/last/pallas_call | solution.py:221
  102.4 0.0 all-to-all-done.3.first_ref
  102.4 29.4 %all_to_all.26.rest_ref = bf16[8,384,128]{2,1,0:T(8,128)(2,1)} all-to-all(bf16[8,384,128]{2,1,0:T(8,128)(2,1)} %last.1), channel_id=1, replica_groups=mesh['wide'=32,'narrow'=8] {'narrow'}, dimensions={0} | all-to-all | bytes 1572864 | tf_op jit(solution)/shard_map/all_to_all | solution.py:224
  131.8 3.3 %join.1 = f32[4096,128]{1,0:T(8,128)} custom-call(bf16[8,128,128]{2,1,0:T(8,128)(2,1)} %copy-done, bf16[8,384,128]{2,1,0:T(8,128)(2,1)} %all_to_all.26.rest_ref), custom_call_target="tpu_custom_call" | custom-call | flops 1073741824 | bytes 4194304 | tf_op jit(solution)/shard_map/join/pallas_call | solution.py:225
  (7 shorter events, 0.1 us)
Async XLA Ops:
  17.6 14.3 %all-to-all-start.1 = ((bf16[16,8,1024]{2,1,0:T(8,128)(2,1)}), bf16[16,8,1024]{2,1,0:T(8,128)(2,1)S(1)}, u32[]{:S(2)}, u32[]{:S(2)}) async-start(bf16[16,8,1024]{2,1,0:T(8,128)(2,1)} %broadcast_in_dim.24), calls=%async_computation.1 | async-start | bytes 524288 | tf_op jit(solution)/shard_map/all_to_all | solution.py:186
  32.8 14.6 %all-to-all-start.2 = ((bf16[16,3,8,1024]{3,2,1,0:T(8,128)(2,1)}), bf16[16,3,8,1024]{3,2,1,0:T(8,128)(2,1)S(1)}, u32[]{:S(2)}, u32[]{:S(2)}) async-start(bf16[16,3,8,1024]{3,2,1,0:T(8,128)(2,1)} %broadcast_in_dim.25), calls=%async_computation.2 | async-start | bytes 1572864 | tf_op jit(solution)/shard_map/all_to_all | solution.py:186
  36.5 10.0 %collective-permute-start = (bf16[16,8,1024]{2,1,0:T(8,128)(2,1)S(1)}, bf16[16,8,1024]{2,1,0:T(8,128)(2,1)S(1)}, u32[]{:S(2)}, u32[]{:S(2)}) collective-permute-start(bf16[16,8,1024]{2,1,0:T(8,128)(2,1)S(1)} %all-to-all-done.1), channel_id=1, source_target_pairs={{0,8},{8,0},{16,24},{24,16},{32,40},{40,32},{48,56},{56,48},{64,72... | collective-permute-start | bytes 786440 | tf_op jit(solution)/shard_map/ppermute | solution.py:201
  47.5 18.1 %collective-permute-start.1 = (bf16[16,3,8,1024]{3,2,1,0:T(8,128)(2,1)S(1)}, bf16[16,3,8,1024]{3,2,1,0:T(8,128)(2,1)S(1)}, u32[]{:S(2)}, u32[]{:S(2)}) collective-permute-start(bf16[16,3,8,1024]{3,2,1,0:T(8,128)(2,1)S(1)} %all-to-all-done.2), channel_id=1, source_target_pairs={{0,8},{8,0},{16,24},{24,16},{32,40},{40,32},{48,56},{56,48},{64,72... | collective-permute-start | bytes 2359304 | tf_op jit(solution)/shard_map/ppermute | solution.py:201
  76.6 25.9 %all-to-all-start.3 = ((bf16[8,128,128]{2,1,0:T(8,128)(2,1)}), bf16[8,128,128]{2,1,0:T(8,128)(2,1)S(1)}, u32[]{:S(2)}, u32[]{:S(2)}) async-start(bf16[8,128,128]{2,1,0:T(8,128)(2,1)} %get-tuple-element.18), calls=%async_computation.3 | async-start | bytes 524288 | tf_op jit(solution)/shard_map/all_to_all | solution.py:219
  102.4 29.4 %copy-start = (bf16[8,128,128]{2,1,0:T(8,128)(2,1)}, bf16[8,128,128]{2,1,0:T(8,128)(2,1)S(1)}, u32[]{:S(2)}) copy-start(bf16[8,128,128]{2,1,0:T(8,128)(2,1)S(1)} %all-to-all-done.3.first_ref) | copy-start | bytes 786436

commit v2 on v1

v2 whole, which is shorter than its diff:
```python
import functools

import jax
import jax.numpy as jnp
from jax import lax
from jax.experimental import pallas as pl
from jax.experimental.pallas import tpu as pltpu
from jax.sharding import PartitionSpec as P

PB = 256
F32 = jnp.float32
BF16 = jnp.bfloat16


def mm(a, b):
    return jnp.dot(a, b, preferred_element_type=F32)


def mm_nt(a, b):
    return lax.dot_general(a, b, (((1,), (1,)), ((), ())), preferred_element_type=F32)


def square(x):
    return x * x


def split(x):
    high = x.astype(BF16)
    return high, (x - high.astype(F32)).astype(BF16)


def fmm(a, b):
    (ah, al), (bh, bl) = split(a), split(b)
    return mm(ah, bh) + (mm(ah, bl) + mm(al, bh))


def fmm_nt(a, b):
    (ah, al), (bh, bl) = split(a), split(b)
    return mm_nt(ah, bh) + (mm_nt(ah, bl) + mm_nt(al, bh))


def over_lanes(x, j):
    return jnp.broadcast_to(x[:, j : j + 1], x.shape)


def over_rows(x, m):
    return jnp.broadcast_to(x[m : m + 1, :], x.shape)


def inverse_factor(matrix, store, between):
    n = matrix.shape[1]
    tiles = [matrix[8 * i : 8 * i + 8, :] for i in range(n // 8)]
    row = lax.broadcasted_iota(jnp.int32, (8, n), 0)
    lane = lax.broadcasted_iota(jnp.int32, (8, n), 1)
    one = tiles[0] * 0.0 + 1.0
    for b in range(n // 8):
        pivot = tiles[b]
        cols = [over_lanes(pivot, 8 * b + m) * one for m in range(8)]
        result = jnp.zeros((8, n), F32)
        for m in range(8):
            j = 8 * b + m
            d = over_rows(cols[m], m)
            r = 1.0 / d
            here = row == m
            mult = jnp.where(here, -r, cols[m] * r)
            prow = jnp.where(lane == j, 1.0, over_rows(pivot, m))
            result = jnp.where(here & (lane <= j), prow * lax.rsqrt(d), result)
            pivot = jnp.where(here | (lane == j), 0.0, pivot) - mult * prow
            for k in range(m + 1, 8):
                cols[k] = jnp.where(here, 0.0, cols[k]) - mult * over_rows(cols[k], m)
        store(b, result)
        between()
        if b + 1 < n // 8:
            rows = [over_rows(pivot, m) for m in range(8)]
            keep = (lane // 8) != b
            for i in range(b + 1, n // 8):
                t = [over_lanes(tiles[i], 8 * b + m) * rows[m] for m in range(8)]
                t = ((t[0] + t[1]) + (t[2] + t[3])) + ((t[4] + t[5]) + (t[6] + t[7]))
                tiles[i] = jnp.where(keep, tiles[i], 0.0) - t


def factor_block(block, out_ref, jobs, half=128):
    jobs = list(jobs)
    steps = 2 * half // 8
    count = [0, 0]

    def between():
        count[0] += 1
        while count[1] < len(jobs) and count[1] * (steps - 2) < count[0] * len(jobs):
            jobs[count[1]]()
            count[1] += 1

    def writer(base):
        def store(i, tile):
            out_ref[base + 8 * i : base + 8 * i + 8, base : base + half] = tile

        return store

    out_ref[:half, half:] = jnp.zeros((half, half), F32)
    inverse_factor(block[:half, :half], writer(0), between)
    top = out_ref[:half, :half]
    lower = fmm_nt(block[half:, :half], top)
    inverse_factor(block[half:, half:] - fmm_nt(lower, lower), writer(half), between)
    out_ref[half:, :half] = -fmm(out_ref[half:, half:], fmm(lower, top))


def own_kernel(rows_ref, metric_ref, proj_ref, spread_ref, spread_t_ref):
    proj_ref[...] = mm(rows_ref[...], metric_ref[...]).astype(BF16)
    for ref, cols in ((spread_ref, 256), (spread_t_ref, 512)):
        per = cols // 8
        r = lax.broadcasted_iota(jnp.int32, (1024, 1024), 0)
        c = lax.broadcasted_iota(jnp.int32, (1024, 1024), 1)
        dst, lane = c // 128, c % 128
        want = (lane // per) * cols + (lane % per) * 8 + dst
        ref[...] = jnp.where(r == want, 1.0, 0.0).astype(BF16)


def first_kernel(panel_ref, metric_ref, own_proj_ref, inv_ref, head_ref, own_ref, proj_ref):
    proj_ref[:PB] = mm(panel_ref[:PB], metric_ref[...]).astype(BF16)
    diag = square(mm_nt(proj_ref[:PB], panel_ref[:PB]))

    def project():
        proj_ref[PB:] = mm(panel_ref[PB : 2 * PB], metric_ref[...]).astype(BF16)

    def slab(out, rows, r, c):
        def job():
            out[r : r + PB, c : c + PB] = square(
                mm_nt(rows[r : r + PB], panel_ref[c : c + PB])
            )

        return job

    jobs = [project]
    jobs += [slab(own_ref, own_proj_ref, r, c) for c in range(0, 1024, PB) for r in (0, PB)]
    jobs += [slab(head_ref, proj_ref, r, c) for r in (0, PB) for c in range(0, 1024, PB) if r + c]
    factor_block(0.5 * (diag + diag.T), inv_ref, jobs)


def packed(values, groups, spread):
    size = values.shape[0] // groups
    side = jnp.concatenate([values[g * size : (g + 1) * size] for g in range(groups)], axis=1)
    return mm(side.astype(BF16), spread).astype(BF16)


def second_kernel(inv0_ref, head_ref, own_ref, inv_ref, own1_ref, upper1_ref, col_ref, upper_ref):
    inv0 = inv0_ref[...]
    upper_ref[:, :PB] = fmm(inv0, head_ref[:PB, PB : 2 * PB])
    low = fmm_nt(head_ref[PB:, :PB], inv0)
    diag = head_ref[PB:, PB : 2 * PB] - fmm(low, upper_ref[:, :PB])

    def column(r):
        def job():
            col_ref[r : r + PB] = fmm_nt(own_ref[r : r + PB, :PB], inv0)

        return job

    def top(c):
        def job():
            upper_ref[:, c : c + PB] = fmm(inv0, head_ref[:PB, PB + c : 2 * PB + c])

        return job

    def under(c):
        def job():
            upper1_ref[:, c - PB : c] = head_ref[PB:, PB + c : 2 * PB + c] - fmm(
                low, upper_ref[:, c : c + PB]
            )

        return job

    def rest(r, c):
        def job():
            own1_ref[r : r + PB, c : c + PB] = own_ref[r : r + PB, PB + c : 2 * PB + c] - fmm(
                col_ref[r : r + PB], upper_ref[:, c : c + PB]
            )

        return job

    jobs = [column(0), column(PB), top(PB), top(2 * PB), under(PB), under(2 * PB)]
    jobs += [rest(r, c) for c in range(0, 768, PB) for r in (0, PB)]
    factor_block(0.5 * (diag + diag.T), inv_ref, jobs)


def last_kernel(own1_ref, upper1_ref, col_ref, inv_ref, spread_ref, spread_t_ref, send_ref):
    inv = inv_ref[...]
    col = fmm_nt(own1_ref[:, :PB], inv)
    upper = fmm(inv, upper1_ref[...])
    trail = packed(own1_ref[:, PB:] - fmm(col, upper), 2, spread_t_ref[...])
    first = packed(col_ref[...], 4, spread_ref[...])
    strips = packed(col, 4, spread_ref[...])
    for s in range(8):
        send_ref[s, :128] = first[:, 128 * s : 128 * s + 128]
        send_ref[s, 128:256] = strips[:, 128 * s : 128 * s + 128]
        send_ref[s, 256:] = trail[:, 128 * s : 128 * s + 128]


def join_kernel(got_ref, out_ref):
    group = pl.program_id(0)
    lane = lax.broadcasted_iota(jnp.int32, (128, 128), 1)
    for s in range(8):
        a, b = got_ref[s, :128].astype(F32), got_ref[s, 128:256].astype(F32)
        t = got_ref[s, pl.ds(256 + 128 * (group % 2), 128)].astype(F32)
        x = pltpu.roll(a, (128 - 32 * group) % 128, 1)
        y = pltpu.roll(b, (160 - 32 * group) % 128, 1)
        z = pltpu.roll(t, (192 - 64 * (group // 2)) % 128, 1)
        out_ref[pl.ds(s, 128, stride=8), :] = jnp.where(
            lane < 32, x, jnp.where(lane < 64, y, z)
        )


def call(kernel, outs, flops, name, scratch=(), **more):
    shapes = [jax.ShapeDtypeStruct(s, t) for s, t in outs]
    return pl.pallas_call(
        kernel,
        out_shape=shapes[0] if len(shapes) == 1 else shapes,
        scratch_shapes=[pltpu.VMEM(s, t) for s, t in scratch],
        name=name,
        compiler_params=pltpu.CompilerParams(vmem_limit_bytes=56 << 20),
        cost_estimate=pl.CostEstimate(flops=flops, bytes_accessed=4 << 20, transcendentals=0),
        **more,
    )


def spread_to(value, count, axis, groups=None):
    wide = jnp.broadcast_to(value[None], (count,) + value.shape)
    return lax.all_to_all(wide, axis, 0, 0, tiled=True, axis_index_groups=groups)


def local(constraint_rows, metric):
    cores = 2
    plane = lax.axis_size("wide") // cores
    narrow = lax.axis_size("narrow")
    same_core = [[cores * i + c for i in range(plane)] for c in range(cores)]
    swap = [(i, i ^ 1) for i in range(plane * cores)]
    core = lax.axis_index("wide") % cores
    rows = constraint_rows[:, 0, :]
    row_count, n = rows.shape

    def gathered(block):
        mine = spread_to(block, plane, "wide", same_core)
        other = lax.ppermute(mine, "wide", swap)
        return jnp.where(
            core == 0, jnp.stack([mine, other], 1), jnp.stack([other, mine], 1)
        )

    column = spread_to(rows[:4], narrow, "narrow").transpose(1, 0, 2)
    own_proj, spread, spread_t = call(
        own_kernel, [((row_count, n), BF16), ((1024, 1024), BF16), ((1024, 1024), BF16)], 8 << 30, "own"
    )(rows, metric)
    mine = spread_to(column, plane, "wide", same_core)
    mine, own_proj = lax.optimization_barrier((mine, own_proj))
    other = lax.ppermute(mine, "wide", swap)
    panel = jnp.where(core == 0, jnp.stack([mine, other], 1), jnp.stack([other, mine], 1))
    panel = panel.transpose(2, 0, 1, 3, 4).reshape(4 * PB, n)
    inv0, head, own = call(
        first_kernel,
        [((PB, PB), F32), ((2 * PB, 4 * PB), F32), ((row_count, 4 * PB), F32)],
        16 << 30, "first", [((2 * PB, n), BF16)],
    )(panel, metric, own_proj)
    inv1, own1, upper1, col = call(
        second_kernel,
        [((PB, PB), F32), ((row_count, 3 * PB), F32), ((PB, 2 * PB), F32), ((row_count, PB), F32)],
        16 << 30, "second", [((PB, 3 * PB), F32)],
    )(inv0, head, own)
    send = call(last_kernel, [((8, 512, 128), BF16)], 4 << 30, "last")(
        own1, upper1, col, inv1, spread, spread_t
    )
    got = lax.all_to_all(send, "narrow", 0, 0, tiled=True)
    out = call(
        join_kernel, [((row_count * 8, 128), F32)], 1 << 30, "join",
        grid=(4,), in_specs=[pl.BlockSpec((8, 512, 128), lambda g: (0, 0, 0))],
        out_specs=pl.BlockSpec((1024, 128), lambda g: (g, 0)),
    )(got)
    return out.reshape(row_count, 8, 1, 128)


def solution(mesh):
    placed = (P(None, ("wide", "narrow"), None), P())
    return jax.shard_map(
        local,
        mesh=mesh,
        in_specs=placed,
        out_specs=P(None, "wide", "narrow", None),
        check_vma=False,
    )
```

time: 136 us -> 117 us (0.86)
  Pallas kernels: 55 us -> 41.8 us
  starting transfers between devices: 22 us -> 10.3 us
  blocking collectives: 45.5 us -> 49.4 us
  waiting for transfers between devices: 7.62 us -> 10.9 us
    pallas_call x5 -> x4, Pallas kernels: 48.7 us -> 35.4 us  [the longest x1 12.8 us: local(): call(first_kernel, [((PB, PB), F32), ((2 * PB, 4 * PB), F32), ((row_count...]
    ppermute x2 -> x1, starting transfers between devices: 8 us -> 3.55 us  [local(): other = lax.ppermute(mine, 'wide', swap)]
    all_to_all x1, blocking collectives: 29.4 us -> 33.4 us  [local(): got = lax.all_to_all(send, 'narrow', 0, 0, tiled=True)]
    all_to_all x1 -> x0, starting transfers between devices: 3.63 us -> none  [local(): got0 = lax.all_to_all(send0, 'narrow', 0, 0, tiled=True)]
    all_to_all x2 -> x1, starting transfers between devices: 10.4 us -> 6.75 us  [spread_to(): lax.all_to_all(wide, axis, 0, 0, tiled=True, axis_index_groups=groups)]
    ppermute x2 -> x1, waiting for transfers between devices: 0.01 us -> 2.29 us  [local(): other = lax.ppermute(mine, 'wide', swap)]
    all_to_all x2 -> x1, waiting for transfers between devices: 7.61 us -> 8.62 us  [spread_to(): lax.all_to_all(wide, axis, 0, 0, tiled=True, axis_index_groups=groups)]
  transfers between devices with their start and end apart: 5 -> 2, of which waited for: 2 -> 2; matrix products, arithmetic and copies ran while one was open for 1% -> 0% of each run, Pallas kernels for 31% -> 5%
where the time goes in v2:
time: 117 us; the launch traced here: 116 us
  blocking collectives  49.4 us (42%)
  Pallas kernels  41.8 us (36%)
  waiting for transfers between devices  10.9 us (9%)
  starting transfers between devices  10.3 us (9%)
  local copies, waits for them, and re-layouts  3.43 us (3%)
    all_to_all x1, blocking collectives, local(): got = lax.all_to_all(send, 'narrow', 0, 0, tiled=True)  33.4 us
    all_to_all x1, blocking collectives, spread_to(): lax.all_to_all(wide, axis, 0, 0, tiled=True, axis_index_groups=groups)  16 us
    pallas_call x1, Pallas kernels, local(): call(first_kernel, [((PB, PB), F32), ((2 * PB, 4 * PB), F32), ((row_count...  12.8 us
    pallas_call x1, Pallas kernels, local(): call(second_kernel, [((PB, PB), F32), ((row_count, 3 * PB), F32), ((PB, 2...  12.5 us
    all_to_all x1, waiting for transfers between devices, spread_to(): lax.all_to_all(wide, axis, 0, 0, tiled=True, axis_index_groups=groups)  8.62 us
    all_to_all x1, starting transfers between devices, spread_to(): lax.all_to_all(wide, axis, 0, 0, tiled=True, axis_index_groups=groups)  6.75 us
    pallas_call x1, Pallas kernels, local(): call(own_kernel, [((row_count, n), BF16), ((1024, 1024), BF16), ((1024, 1...  6.33 us
    pallas_call x1, Pallas kernels, local(): call(last_kernel, [((8, 512, 128), BF16)], 4 << 30, 'last')  6.27 us
  transfers between devices with their start and end apart: 2, of which 2 were waited for; matrix products, arithmetic and copies ran while one was open for 0% of the time, Pallas kernels for 5%

profile of v2, /device:TPU:1, one launch (start us, length us, event | category | flops | bytes accessed | tf_op | source)
XLA Modules:
  0.0 116.2 jit_solution(9909045500810481956)
XLA Ops:
  0.0 0.7 slice_bitcast_fusion
  0.7 16.0 %all_to_all.15 = bf16[8,4,1024]{2,1,0:T(4,128)(2,1)S(1)} all-to-all(bf16[8,4,1024]{2,1,0:T(4,128)(2,1)S(1)} %broadcast_in_dim.7), channel_id=1, replica_groups=mesh['wide'=32,'narrow'=8] {'narrow'}, dimensions={0} | all-to-all | bytes 131072 | tf_op jit(solution)/shard_map/all_to_all | solution.py:226
  16.8 1.1 broadcast_in_dim.16
  17.9 6.8 %all-to-all-start.1 = ((bf16[16,4,8,1024]{3,2,1,0:T(8,128)(2,1)}), bf16[16,4,8,1024]{3,2,1,0:T(8,128)(2,1)S(1)}, u32[]{:S(2)}, u32[]{:S(2)}) async-start(bf16[16,4,8,1024]{3,2,1,0:T(8,128)(2,1)} %broadcast_in_dim.16), calls=%async_computation.1 | async-start | bytes 2097152 | tf_op jit(solution)/shard_map/all_to_all | solution.py:226
  24.7 6.3 %own.1 = (bf16[512,1024]{1,0:T(8,128)(2,1)}, bf16[1024,1024]{1,0:T(8,128)(2,1)}, bf16[1024,1024]{1,0:T(8,128)(2,1)}) custom-call(bf16[512,1024]{1,0:T(8,128)(2,1)} %bitcast.16, bf16[1024,1024]{1,0:T(8,128)(2,1)} %metric_ref.3), custom_call_target="tpu_custom_call" | custom-call | flops 8589934592 | bytes 4194304 | tf_op jit(solution)/shard_map/own/pallas_call | solution.py:247
  31.0 8.6 %all-to-all-done.1 = bf16[16,4,8,1024]{3,2,1,0:T(8,128)(2,1)S(1)} async-done(((bf16[16,4,8,1024]{3,2,1,0:T(8,128)(2,1)}), bf16[16,4,8,1024]{3,2,1,0:T(8,128)(2,1)S(1)}, u32[]{:S(2)}, u32[]{:S(2)}) %all-to-all-start.1) | async-done | bytes 1048608 | tf_op jit(solution)/shard_map/all_to_all | solution.py:226
  39.6 3.5 %collective-permute-start = (bf16[16,4,8,1024]{3,2,1,0:T(8,128)(2,1)S(1)}, bf16[16,4,8,1024]{3,2,1,0:T(8,128)(2,1)S(1)}, u32[]{:S(2)}, u32[]{:S(2)}) collective-permute-start(bf16[16,4,8,1024]{3,2,1,0:T(8,128)(2,1)S(1)} %all-to-all-done.1), channel_id=1, source_target_pairs={{0,8},{8,0},{16,24},{24,16},{32,40},{40,32},{48,56},{56,48},{64,72... | collective-permute-start | bytes 3145736 | tf_op jit(solution)/shard_map/ppermute | solution.py:252
  43.2 2.3 %collective-permute-done = bf16[16,4,8,1024]{3,2,1,0:T(8,128)(2,1)S(1)} collective-permute-done((bf16[16,4,8,1024]{3,2,1,0:T(8,128)(2,1)S(1)}, bf16[16,4,8,1024]{3,2,1,0:T(8,128)(2,1)S(1)}, u32[]{:S(2)}, u32[]{:S(2)}) %collective-permute-start) | collective-permute-done | bytes 1048608 | tf_op jit(solution)/shard_map/ppermute | solution.py:252
  45.5 0.3 fusion
  45.8 1.6 %copy.5 = bf16[4,16,2,8,1024]{4,3,2,1,0:T(8,128)(2,1)} copy(bf16[4,16,2,8,1024]{4,3,0,1,2:T(8,128)(2,1)S(1)} %fusion) | data formatting | bytes 4194304 | tf_op jit(solution)/shard_map/transpose | solution.py:254
  47.4 12.8 %first.1 = (f32[256,256]{1,0:T(8,128)}, f32[512,1024]{1,0:T(8,128)}, f32[512,1024]{1,0:T(8,128)}) custom-call(bf16[1024,1024]{1,0:T(8,128)(2,1)} %bitcast.13, bf16[1024,1024]{1,0:T(8,128)(2,1)} %metric_ref.3, bf16[512,1024]{1,0:T(8,128)(2,1)} %get-tuple-element.19.own_proj_ref), custom_call_target="tpu_custom_call" | custom-call | flops 17179869184 | bytes 4194304 | tf_op jit(solution)/shard_map/first/pallas_call | solution.py:255
  60.2 12.5 %second.1 = (f32[256,256]{1,0:T(8,128)}, f32[512,768]{1,0:T(8,128)}, f32[256,512]{1,0:T(8,128)}, f32[512,256]{1,0:T(8,128)}) custom-call(f32[256,256]{1,0:T(8,128)} %get-tuple-element.20.inv0_ref, f32[512,1024]{1,0:T(8,128)} %get-tuple-element.21.head_ref, f32[512,1024]{1,0:T(8,128)} %get-tuple-element.22.own_ref), custom_call_target="tpu_custom_call" | custom-call | flops 17179869184 | bytes 4194304 | tf_op jit(solution)/shard_map/second/pallas_call | solution.py:260
  72.7 6.3 %last.1 = bf16[8,512,128]{2,1,0:T(8,128)(2,1)} custom-call(f32[512,768]{1,0:T(8,128)} %get-tuple-element.23.own1_ref, f32[256,512]{1,0:T(8,128)} %get-tuple-element.24.upper1_ref, f32[512,256]{1,0:T(8,128)} %get-tuple-element.25.col_ref, f32[256,256]{1,0:T(8,128)} %get-tuple-element.26.inv_ref, bf16[1024,1024]{1,0:T(8,128)(2,1)} %get-tuple-element.27.spread_ref, ...), custom_call_target="tpu_custom_call" | custom-call | flops 4294967296 | bytes 4194304 | tf_op jit(solution)/shard_map/last/pallas_call | solution.py:265
  79.0 33.4 %all_to_all.16.got_ref = bf16[8,512,128]{2,1,0:T(8,128)(2,1)} all-to-all(bf16[8,512,128]{2,1,0:T(8,128)(2,1)} %last.1), channel_id=1, replica_groups=mesh['wide'=32,'narrow'=8] {'narrow'}, dimensions={0} | all-to-all | bytes 2097152 | tf_op jit(solution)/shard_map/all_to_all | solution.py:268
  112.4 3.8 %join.1 = f32[4096,128]{1,0:T(8,128)} custom-call(bf16[8,512,128]{2,1,0:T(8,128)(2,1)} %all_to_all.16.got_ref), custom_call_target="tpu_custom_call" | custom-call | flops 1073741824 | bytes 4194304 | tf_op jit(solution)/shard_map/join/pallas_call | solution.py:269
  (2 shorter events, 0.0 us)
Async XLA Ops:
  17.9 21.7 %all-to-all-start.1 = ((bf16[16,4,8,1024]{3,2,1,0:T(8,128)(2,1)}), bf16[16,4,8,1024]{3,2,1,0:T(8,128)(2,1)S(1)}, u32[]{:S(2)}, u32[]{:S(2)}) async-start(bf16[16,4,8,1024]{3,2,1,0:T(8,128)(2,1)} %broadcast_in_dim.16), calls=%async_computation.1 | async-start | bytes 2097152 | tf_op jit(solution)/shard_map/all_to_all | solution.py:226
  39.6 5.8 %collective-permute-start = (bf16[16,4,8,1024]{3,2,1,0:T(8,128)(2,1)S(1)}, bf16[16,4,8,1024]{3,2,1,0:T(8,128)(2,1)S(1)}, u32[]{:S(2)}, u32[]{:S(2)}) collective-permute-start(bf16[16,4,8,1024]{3,2,1,0:T(8,128)(2,1)S(1)} %all-to-all-done.1), channel_id=1, source_target_pairs={{0,8},{8,0},{16,24},{24,16},{32,40},{40,32},{48,56},{56,48},{64,72... | collective-permute-start | bytes 3145736 | tf_op jit(solution)/shard_map/ppermute | solution.py:252

commit v3 on v2

--- a/solution.py
+++ b/solution.py
@@ -115,34 +115,55 @@
         ref[...] = jnp.where(r == want, 1.0, 0.0).astype(BF16)
 
 
-def first_kernel(panel_ref, metric_ref, own_proj_ref, inv_ref, head_ref, own_ref, proj_ref):
-    proj_ref[:PB] = mm(panel_ref[:PB], metric_ref[...]).astype(BF16)
-    diag = square(mm_nt(proj_ref[:PB], panel_ref[:PB]))
-
-    def project():
-        proj_ref[PB:] = mm(panel_ref[PB : 2 * PB], metric_ref[...]).astype(BF16)
-
-    def slab(out, rows, r, c):
-        def job():
-            out[r : r + PB, c : c + PB] = square(
-                mm_nt(rows[r : r + PB], panel_ref[c : c + PB])
-            )
-
-        return job
-
-    jobs = [project]
-    jobs += [slab(own_ref, own_proj_ref, r, c) for c in range(0, 1024, PB) for r in (0, PB)]
-    jobs += [slab(head_ref, proj_ref, r, c) for r in (0, PB) for c in range(0, 1024, PB) if r + c]
-    factor_block(0.5 * (diag + diag.T), inv_ref, jobs)
-
-
 def packed(values, groups, spread):
     size = values.shape[0] // groups
     side = jnp.concatenate([values[g * size : (g + 1) * size] for g in range(groups)], axis=1)
     return mm(side.astype(BF16), spread).astype(BF16)
 
 
-def second_kernel(inv0_ref, head_ref, own_ref, inv_ref, own1_ref, upper1_ref, col_ref, upper_ref):
+def core_kernel(
+    core_ref, mine_ref, other_ref, metric_hbm, own_proj_hbm, spread_hbm, spread_t_hbm, send_ref,
+    panel_ref, metric_ref, own_proj_ref, spread_ref, spread_t_ref, proj_ref, head_ref, own_ref,
+    own1_ref, upper_ref, upper1_ref, col_ref, inv0_ref, inv1_ref, sems,
+):
+    pairs = (
+        (metric_hbm, metric_ref), (own_proj_hbm, own_proj_ref),
+        (spread_hbm, spread_ref), (spread_t_hbm, spread_t_ref),
+    )
+    copies = [pltpu.make_async_copy(x, y, sems.at[i]) for i, (x, y) in enumerate(pairs)]
+    for copy in copies:
+        copy.start()
+    first_core = core_ref[0] == 0
+    for k in range(4):
+        for i in range(16):
+            x, y = mine_ref[i, k].astype(F32), other_ref[i, k].astype(F32)
+            low, high = jnp.where(first_core, x, y), jnp.where(first_core, y, x)
+            panel_ref[256 * k + 16 * i : 256 * k + 16 * i + 16] = jnp.concatenate(
+                [low, high], axis=0
+            ).astype(BF16)
+    copies[0].wait()
+    proj_ref[:PB] = mm(panel_ref[:PB], metric_ref[...]).astype(BF16)
+    diag = square(mm_nt(proj_ref[:PB], panel_ref[:PB]))
+    copies[1].wait()
+
+    def project():
+        proj_ref[PB:] = mm(panel_ref[PB : 2 * PB], metric_ref[...]).astype(BF16)
+
+    def slab(out, rows, r, c):
+        def job():
+            out[r : r + PB, c : c + PB] = square(
+                mm_nt(rows[r : r + PB], panel_ref[c : c + PB])
+            )
+
+        return job
+
+    jobs = [project]
+    jobs += [slab(own_ref, own_proj_ref, r, c) for c in range(0, 1024, PB) for r in (0, PB)]
+    jobs += [slab(head_ref, proj_ref, r, c) for r in (0, PB) for c in range(0, 1024, PB) if r + c]
+    factor_block(0.5 * (diag + diag.T), inv0_ref, jobs)
+    copies[2].wait()
+    copies[3].wait()
+
     inv0 = inv0_ref[...]
     upper_ref[:, :PB] = fmm(inv0, head_ref[:PB, PB : 2 * PB])
     low = fmm_nt(head_ref[PB:, :PB], inv0)
@@ -176,20 +197,21 @@
 
         return job
 
+    def finished():
+        strips = packed(col_ref[...], 4, spread_ref[...])
+        for s in range(8):
+            send_ref[s, :128] = strips[:, 128 * s : 128 * s + 128]
+
     jobs = [column(0), column(PB), top(PB), top(2 * PB), under(PB), under(2 * PB)]
-    jobs += [rest(r, c) for c in range(0, 768, PB) for r in (0, PB)]
-    factor_block(0.5 * (diag + diag.T), inv_ref, jobs)
-
-
-def last_kernel(own1_ref, upper1_ref, col_ref, inv_ref, spread_ref, spread_t_ref, send_ref):
-    inv = inv_ref[...]
+    jobs += [rest(r, c) for c in range(0, 768, PB) for r in (0, PB)] + [finished]
+    factor_block(0.5 * (diag + diag.T), inv1_ref, jobs)
+
+    inv = inv1_ref[...]
     col = fmm_nt(own1_ref[:, :PB], inv)
     upper = fmm(inv, upper1_ref[...])
     trail = packed(own1_ref[:, PB:] - fmm(col, upper), 2, spread_t_ref[...])
-    first = packed(col_ref[...], 4, spread_ref[...])
     strips = packed(col, 4, spread_ref[...])
     for s in range(8):
-        send_ref[s, :128] = first[:, 128 * s : 128 * s + 128]
         send_ref[s, 128:256] = strips[:, 128 * s : 128 * s + 128]
         send_ref[s, 256:] = trail[:, 128 * s : 128 * s + 128]
 
@@ -197,25 +219,26 @@
 def join_kernel(got_ref, out_ref):
     group = pl.program_id(0)
     lane = lax.broadcasted_iota(jnp.int32, (128, 128), 1)
+    parts = []
     for s in range(8):
         a, b = got_ref[s, :128].astype(F32), got_ref[s, 128:256].astype(F32)
         t = got_ref[s, pl.ds(256 + 128 * (group % 2), 128)].astype(F32)
         x = pltpu.roll(a, (128 - 32 * group) % 128, 1)
         y = pltpu.roll(b, (160 - 32 * group) % 128, 1)
         z = pltpu.roll(t, (192 - 64 * (group // 2)) % 128, 1)
-        out_ref[pl.ds(s, 128, stride=8), :] = jnp.where(
-            lane < 32, x, jnp.where(lane < 64, y, z)
-        )
-
-
-def call(kernel, outs, flops, name, scratch=(), **more):
+        parts.append(jnp.where(lane < 32, x, jnp.where(lane < 64, y, z)))
+    stacked = jnp.stack(parts, 0)
+    out_ref[...] = pltpu.einshape("skl->ksl", stacked).reshape(1024, 128)
+
+
+def call(kernel, outs, flops, name, scratch=(), sems=(), **more):
     shapes = [jax.ShapeDtypeStruct(s, t) for s, t in outs]
     return pl.pallas_call(
         kernel,
         out_shape=shapes[0] if len(shapes) == 1 else shapes,
-        scratch_shapes=[pltpu.VMEM(s, t) for s, t in scratch],
+        scratch_shapes=[pltpu.VMEM(s, t) for s, t in scratch] + list(sems),
         name=name,
-        compiler_params=pltpu.CompilerParams(vmem_limit_bytes=56 << 20),
+        compiler_params=pltpu.CompilerParams(vmem_limit_bytes=48 << 20),
         cost_estimate=pl.CostEstimate(flops=flops, bytes_accessed=4 << 20, transcendentals=0),
         **more,
     )
@@ -250,21 +273,18 @@
     mine = spread_to(column, plane, "wide", same_core)
     mine, own_proj = lax.optimization_barrier((mine, own_proj))
     other = lax.ppermute(mine, "wide", swap)
-    panel = jnp.where(core == 0, jnp.stack([mine, other], 1), jnp.stack([other, mine], 1))
-    panel = panel.transpose(2, 0, 1, 3, 4).reshape(4 * PB, n)
-    inv0, head, own = call(
-        first_kernel,
-        [((PB, PB), F32), ((2 * PB, 4 * PB), F32), ((row_count, 4 * PB), F32)],
-        16 << 30, "first", [((2 * PB, n), BF16)],
-    )(panel, metric, own_proj)
-    inv1, own1, upper1, col = call(
-        second_kernel,
-        [((PB, PB), F32), ((row_count, 3 * PB), F32), ((PB, 2 * PB), F32), ((row_count, PB), F32)],
-        16 << 30, "second", [((PB, 3 * PB), F32)],
-    )(inv0, head, own)
-    send = call(last_kernel, [((8, 512, 128), BF16)], 4 << 30, "last")(
-        own1, upper1, col, inv1, spread, spread_t
-    )
+    hbm, vmem = pl.BlockSpec(memory_space=pl.ANY), pl.BlockSpec(memory_space=pltpu.VMEM)
+    send = call(
+        core_kernel, [((8, row_count, 128), BF16)], 16 << 30, "core",
+        [
+            ((4 * PB, n), BF16), ((n, n), BF16), ((row_count, n), BF16), ((1024, 1024), BF16),
+            ((1024, 1024), BF16), ((2 * PB, n), BF16), ((2 * PB, 4 * PB), F32),
+            ((row_count, 4 * PB), F32), ((row_count, 3 * PB), F32), ((PB, 3 * PB), F32),
+            ((PB, 2 * PB), F32), ((row_count, PB), F32), ((PB, PB), F32), ((PB, PB), F32),
+        ],
+        [pltpu.SemaphoreType.DMA((4,))],
+        in_specs=[pl.BlockSpec(memory_space=pltpu.SMEM), vmem, vmem, hbm, hbm, hbm, hbm],
+    )(core.reshape(1), mine, other, metric, own_proj, spread, spread_t)
     got = lax.all_to_all(send, "narrow", 0, 0, tiled=True)
     out = call(
         join_kernel, [((row_count * 8, 128), F32)], 1 << 30, "join",

time: 117 us -> 103 us (0.88)
  Pallas kernels: 41.8 us -> 31.6 us
  blocking collectives: 49.4 us -> 47.6 us
    pallas_call x3 -> x1, Pallas kernels: 31.6 us -> 23 us  [local(): call(core_kernel, [((8, row_count, 128), BF16)], 16 << 30, 'core', [((4 *...]
    all_to_all x1, blocking collectives: 33.4 us -> 31.6 us  [local(): got = lax.all_to_all(send, 'narrow', 0, 0, tiled=True)]
    transpose x1 -> x0, local copies, waits for them, and re-layouts: 1.56 us -> none  [local(): panel = panel.transpose(2, 0, 1, 3, 4).reshape(4 * PB, n)]
    unnamed x0 -> x4, local copies, waits for them, and re-layouts: none -> 1.34 us
    pallas_call x1, Pallas kernels: 3.79 us -> 2.59 us  [local(): call(join_kernel, [((row_count * 8, 128), F32)], 1 << 30, 'join', grid=(4...]
  transfers between devices with their start and end apart: 2 -> 2, of which waited for: 2 -> 2; matrix products, arithmetic and copies ran while one was open for 0% -> 0% of each run, Pallas kernels for 5% -> 6%
where the time goes in v3:
time: 103 us
  blocking collectives  47.6 us (46%)
  Pallas kernels  31.6 us (31%)
  starting transfers between devices  10.3 us (10%)
  waiting for transfers between devices  9.84 us (10%)
  local copies, waits for them, and re-layouts  3.31 us (3%)
    all_to_all x1, blocking collectives, local(): got = lax.all_to_all(send, 'narrow', 0, 0, tiled=True)  31.6 us
    pallas_call x1, Pallas kernels, local(): call(core_kernel, [((8, row_count, 128), BF16)], 16 << 30, 'core', [((4 *...  23 us
    all_to_all x1, blocking collectives, spread_to(): lax.all_to_all(wide, axis, 0, 0, tiled=True, axis_index_groups=groups)  16 us
    all_to_all x1, waiting for transfers between devices, spread_to(): lax.all_to_all(wide, axis, 0, 0, tiled=True, axis_index_groups=groups)  7.56 us
    all_to_all x1, starting transfers between devices, spread_to(): lax.all_to_all(wide, axis, 0, 0, tiled=True, axis_index_groups=groups)  6.75 us
    pallas_call x1, Pallas kernels, local(): call(own_kernel, [((row_count, n), BF16), ((1024, 1024), BF16), ((1024, 1...  6.05 us
    ppermute x1, starting transfers between devices, local(): other = lax.ppermute(mine, 'wide', swap)  3.55 us
    pallas_call x1, Pallas kernels, local(): call(join_kernel, [((row_count * 8, 128), F32)], 1 << 30, 'join', grid=(4...  2.59 us
  transfers between devices with their start and end apart: 2, of which 2 were waited for; matrix products, arithmetic and copies ran while one was open for 0% of the time, Pallas kernels for 6%

profile of v3, /device:TPU:1, one launch (start us, length us, event | category | flops | bytes accessed | tf_op | source)
XLA Modules:
  0.0 102.7 jit_solution(5332569566860494295)
XLA Ops:
  0.0 0.0 copy-start
  0.0 0.8 slice_bitcast_fusion
  0.8 16.0 %all_to_all.15 = bf16[8,4,1024]{2,1,0:T(4,128)(2,1)S(1)} all-to-all(bf16[8,4,1024]{2,1,0:T(4,128)(2,1)S(1)} %broadcast_in_dim.7), channel_id=1, replica_groups=mesh['wide'=32,'narrow'=8] {'narrow'}, dimensions={0} | all-to-all | bytes 131072 | tf_op jit(solution)/shard_map/all_to_all | solution.py:249
  16.9 1.1 %broadcast_in_dim.16 = bf16[16,4,8,1024]{3,2,1,0:T(8,128)(2,1)} broadcast(bf16[4,8,1024]{2,1,0:T(8,128)(2,1)S(1)} %copy.4), dimensions={1,2,3} | broadcast | bytes 1114112 | tf_op jit(solution)/shard_map/broadcast_in_dim | solution.py:248
  18.0 6.8 %all-to-all-start.1 = ((bf16[16,4,8,1024]{3,2,1,0:T(8,128)(2,1)}), bf16[16,4,8,1024]{3,2,1,0:T(8,128)(2,1)S(1)}, u32[]{:S(2)}, u32[]{:S(2)}) async-start(bf16[16,4,8,1024]{3,2,1,0:T(8,128)(2,1)} %broadcast_in_dim.16), calls=%async_computation.1 | async-start | bytes 2097152 | tf_op jit(solution)/shard_map/all_to_all | solution.py:249
  24.8 0.0 copy-done
  24.8 6.0 %own.1 = (bf16[512,1024]{1,0:T(8,128)(2,1)S(1)}, bf16[1024,1024]{1,0:T(8,128)(2,1)S(1)}, bf16[1024,1024]{1,0:T(8,128)(2,1)}) custom-call(bf16[512,1024]{1,0:T(8,128)(2,1)S(1)} %bitcast.8, bf16[1024,1024]{1,0:T(8,128)(2,1)} %metric_hbm.1), custom_call_target="tpu_custom_call" | custom-call | flops 8589934592 | bytes 4194304 | tf_op jit(solution)/shard_map/own/pallas_call | solution.py:270
  30.8 0.0 copy-start.1
  30.8 1.3 %copy-done.1 = bf16[1024,1024]{1,0:T(8,128)(2,1)} copy-done((bf16[1024,1024]{1,0:T(8,128)(2,1)}, bf16[1024,1024]{1,0:T(8,128)(2,1)S(1)}, u32[]{:S(2)}) %copy-start.1) | copy-done | bytes 2097176
  32.2 7.6 %all-to-all-done.1.mine_ref = bf16[16,4,8,1024]{3,2,1,0:T(8,128)(2,1)S(1)} async-done(((bf16[16,4,8,1024]{3,2,1,0:T(8,128)(2,1)}), bf16[16,4,8,1024]{3,2,1,0:T(8,128)(2,1)S(1)}, u32[]{:S(2)}, u32[]{:S(2)}) %all-to-all-start.1) | async-done | bytes 1048608 | tf_op jit(solution)/shard_map/all_to_all | solution.py:249
  39.7 3.5 %collective-permute-start = (bf16[16,4,8,1024]{3,2,1,0:T(8,128)(2,1)S(1)}, bf16[16,4,8,1024]{3,2,1,0:T(8,128)(2,1)S(1)}, u32[]{:S(2)}, u32[]{:S(2)}) collective-permute-start(bf16[16,4,8,1024]{3,2,1,0:T(8,128)(2,1)S(1)} %all-to-all-done.1.mine_ref), channel_id=1, source_target_pairs={{0,8},{8,0},{16,24},{24,16},{32,40},{40,32},{48,56},{56,48},{64,72... | collective-permute-start | bytes 3145736 | tf_op jit(solution)/shard_map/ppermute | solution.py:275
  43.3 2.3 %collective-permute-done.other_ref = bf16[16,4,8,1024]{3,2,1,0:T(8,128)(2,1)S(1)} collective-permute-done((bf16[16,4,8,1024]{3,2,1,0:T(8,128)(2,1)S(1)}, bf16[16,4,8,1024]{3,2,1,0:T(8,128)(2,1)S(1)}, u32[]{:S(2)}, u32[]{:S(2)}) %collective-permute-start) | collective-permute-done | bytes 1048608 | tf_op jit(solution)/shard_map/ppermute | solution.py:275
  45.6 23.0 %core.1 = bf16[8,512,128]{2,1,0:T(8,128)(2,1)S(1)} custom-call(s32[1]{0:T(128)} %bitcast.core_ref, bf16[16,4,8,1024]{3,2,1,0:T(8,128)(2,1)S(1)} %all-to-all-done.1.mine_ref, bf16[16,4,8,1024]{3,2,1,0:T(8,128)(2,1)S(1)} %collective-permute-done.other_ref, bf16[1024,1024]{1,0:T(8,128)(2,1)} %metric_hbm.1, ...), custom_call_target="tpu_custom_call" | custom-call | flops 17179869184 | bytes 4194304 | tf_op jit(solution)/shard_map/core/pallas_call | solution.py:277
  68.5 31.6 %all_to_all.16.got_ref = bf16[8,512,128]{2,1,0:T(8,128)(2,1)S(1)} all-to-all(bf16[8,512,128]{2,1,0:T(8,128)(2,1)S(1)} %core.1), channel_id=1, replica_groups=mesh['wide'=32,'narrow'=8] {'narrow'}, dimensions={0} | all-to-all | bytes 2097152 | tf_op jit(solution)/shard_map/all_to_all | solution.py:288
  100.1 2.6 %join.1 = f32[4096,128]{1,0:T(8,128)} custom-call(bf16[8,512,128]{2,1,0:T(8,128)(2,1)S(1)} %all_to_all.16.got_ref), custom_call_target="tpu_custom_call" | custom-call | flops 1073741824 | bytes 4194304 | tf_op jit(solution)/shard_map/join/pallas_call | solution.py:289
  (2 shorter events, 0.0 us)
Async XLA Ops:
  0.0 24.8 %copy-start = (bf16[512,1,1024]{2,0,1:T(8,128)(2,1)S(1)}, bf16[512,1,1024]{2,0,1:T(8,128)(2,1)}, u32[]{:S(2)}) copy-start(bf16[512,1,1024]{2,0,1:T(8,128)(2,1)} %param.2) | copy-start | bytes 3145732
  18.0 21.7 %all-to-all-start.1 = ((bf16[16,4,8,1024]{3,2,1,0:T(8,128)(2,1)}), bf16[16,4,8,1024]{3,2,1,0:T(8,128)(2,1)S(1)}, u32[]{:S(2)}, u32[]{:S(2)}) async-start(bf16[16,4,8,1024]{3,2,1,0:T(8,128)(2,1)} %broadcast_in_dim.16), calls=%async_computation.1 | async-start | bytes 2097152 | tf_op jit(solution)/shard_map/all_to_all | solution.py:249
  30.8 1.3 %copy-start.1 = (bf16[1024,1024]{1,0:T(8,128)(2,1)}, bf16[1024,1024]{1,0:T(8,128)(2,1)S(1)}, u32[]{:S(2)}) copy-start(bf16[1024,1024]{1,0:T(8,128)(2,1)S(1)} %get-tuple-element.13.spread_hbm) | copy-start | bytes 6291460
  39.7 5.8 %collective-permute-start = (bf16[16,4,8,1024]{3,2,1,0:T(8,128)(2,1)S(1)}, bf16[16,4,8,1024]{3,2,1,0:T(8,128)(2,1)S(1)}, u32[]{:S(2)}, u32[]{:S(2)}) collective-permute-start(bf16[16,4,8,1024]{3,2,1,0:T(8,128)(2,1)S(1)} %all-to-all-done.1.mine_ref), channel_id=1, source_target_pairs={{0,8},{8,0},{16,24},{24,16},{32,40},{40,32},{48,56},{56,48},{64,72... | collective-permute-start | bytes 3145736 | tf_op jit(solution)/shard_map/ppermute | solution.py:275

commit v4 on v3

--- a/solution.py
+++ b/solution.py
@@ -47,15 +47,29 @@
     return jnp.broadcast_to(x[m : m + 1, :], x.shape)
 
 
+def tree_sum(terms):
+    while len(terms) > 1:
+        terms = [x + y for x, y in zip(terms[::2], terms[1::2], strict=True)]
+    return terms[0]
+
+
 def inverse_factor(matrix, store, between):
     n = matrix.shape[1]
-    tiles = [matrix[8 * i : 8 * i + 8, :] for i in range(n // 8)]
+    steps = n // 8
+    tiles = [matrix[8 * i : 8 * i + 8, :] for i in range(steps)]
     row = lax.broadcasted_iota(jnp.int32, (8, n), 0)
     lane = lax.broadcasted_iota(jnp.int32, (8, n), 1)
     one = tiles[0] * 0.0 + 1.0
-    for b in range(n // 8):
-        pivot = tiles[b]
-        cols = [over_lanes(pivot, 8 * b + m) * one for m in range(8)]
+
+    def columns(tile, b):
+        return [over_lanes(tile, 8 * b + m) * one for m in range(8)]
+
+    cols = columns(tiles[0], 0)
+    for b in range(steps):
+        pivot, more = tiles[b], b + 1 < steps
+        if more:
+            ahead = columns(pivot, b + 1)
+            below, below_ahead = columns(tiles[b + 1], b), columns(tiles[b + 1], b + 1)
         result = jnp.zeros((8, n), F32)
         for m in range(8):
             j = 8 * b + m
@@ -68,15 +82,23 @@
             pivot = jnp.where(here | (lane == j), 0.0, pivot) - mult * prow
             for k in range(m + 1, 8):
                 cols[k] = jnp.where(here, 0.0, cols[k]) - mult * over_rows(cols[k], m)
+            if more:
+                for k in range(8):
+                    ahead[k] = jnp.where(here, 0.0, ahead[k]) - mult * over_rows(ahead[k], m)
         store(b, result)
         between()
-        if b + 1 < n // 8:
+        if more:
+            cols = [
+                below_ahead[k] - tree_sum([below[m] * over_rows(ahead[k], m) for m in range(8)])
+                for k in range(8)
+            ]
             rows = [over_rows(pivot, m) for m in range(8)]
             keep = (lane // 8) != b
-            for i in range(b + 1, n // 8):
-                t = [over_lanes(tiles[i], 8 * b + m) * rows[m] for m in range(8)]
-                t = ((t[0] + t[1]) + (t[2] + t[3])) + ((t[4] + t[5]) + (t[6] + t[7]))
-                tiles[i] = jnp.where(keep, tiles[i], 0.0) - t
+            for i in range(b + 1, steps):
+                at = below if i == b + 1 else [over_lanes(tiles[i], 8 * b + m) for m in range(8)]
+                tiles[i] = jnp.where(keep, tiles[i], 0.0) - tree_sum(
+                    [at[m] * rows[m] for m in range(8)]
+                )
 
 
 def factor_block(block, out_ref, jobs, half=128):

time: 103 us -> 98.3 us (0.954)
  Pallas kernels: 31.6 us -> 26.9 us
    pallas_call x1, Pallas kernels: 23 us -> 18.3 us  [local(): call(core_kernel, [((8, row_count, 128), BF16)], 16 << 30, 'core', [((4 *...]
where the time goes in v4:
time: 98.3 us; the launch traced here: 98.1 us
  blocking collectives  47.6 us (48%)
  Pallas kernels  26.9 us (27%)
  starting transfers between devices  10.3 us (10%)
  waiting for transfers between devices  9.84 us (10%)
  local copies, waits for them, and re-layouts  3.31 us (3%)
    all_to_all x1, blocking collectives, local(): got = lax.all_to_all(send, 'narrow', 0, 0, tiled=True)  31.6 us
    pallas_call x1, Pallas kernels, local(): call(core_kernel, [((8, row_count, 128), BF16)], 16 << 30, 'core', [((4 *...  18.3 us
    all_to_all x1, blocking collectives, spread_to(): lax.all_to_all(wide, axis, 0, 0, tiled=True, axis_index_groups=groups)  16 us
    all_to_all x1, waiting for transfers between devices, spread_to(): lax.all_to_all(wide, axis, 0, 0, tiled=True, axis_index_groups=groups)  7.56 us
    all_to_all x1, starting transfers between devices, spread_to(): lax.all_to_all(wide, axis, 0, 0, tiled=True, axis_index_groups=groups)  6.75 us
    pallas_call x1, Pallas kernels, local(): call(own_kernel, [((row_count, n), BF16), ((1024, 1024), BF16), ((1024, 1...  6.05 us
    ppermute x1, starting transfers between devices, local(): other = lax.ppermute(mine, 'wide', swap)  3.55 us
    pallas_call x1, Pallas kernels, local(): call(join_kernel, [((row_count * 8, 128), F32)], 1 << 30, 'join', grid=(4...  2.59 us
  transfers between devices with their start and end apart: 2, of which 2 were waited for; matrix products, arithmetic and copies ran while one was open for 0% of the time, Pallas kernels for 6%

profile of v4, /device:TPU:1, one launch (start us, length us, event | category | flops | bytes accessed | tf_op | source)
XLA Modules:
  0.0 98.1 jit_solution(3820847270524338899)
XLA Ops:
  0.0 0.0 copy-start
  0.0 0.8 slice_bitcast_fusion
  0.8 16.0 %all_to_all.15 = bf16[8,4,1024]{2,1,0:T(4,128)(2,1)S(1)} all-to-all(bf16[8,4,1024]{2,1,0:T(4,128)(2,1)S(1)} %broadcast_in_dim.7), channel_id=1, replica_groups=mesh['wide'=32,'narrow'=8] {'narrow'}, dimensions={0} | all-to-all | bytes 131072 | tf_op jit(solution)/shard_map/all_to_all | solution.py:271
  16.9 1.1 %broadcast_in_dim.16 = bf16[16,4,8,1024]{3,2,1,0:T(8,128)(2,1)} broadcast(bf16[4,8,1024]{2,1,0:T(8,128)(2,1)S(1)} %copy.4), dimensions={1,2,3} | broadcast | bytes 1114112 | tf_op jit(solution)/shard_map/broadcast_in_dim | solution.py:270
  18.0 6.8 %all-to-all-start.1 = ((bf16[16,4,8,1024]{3,2,1,0:T(8,128)(2,1)}), bf16[16,4,8,1024]{3,2,1,0:T(8,128)(2,1)S(1)}, u32[]{:S(2)}, u32[]{:S(2)}) async-start(bf16[16,4,8,1024]{3,2,1,0:T(8,128)(2,1)} %broadcast_in_dim.16), calls=%async_computation.1 | async-start | bytes 2097152 | tf_op jit(solution)/shard_map/all_to_all | solution.py:271
  24.8 0.0 copy-done
  24.8 6.0 %own.1 = (bf16[512,1024]{1,0:T(8,128)(2,1)S(1)}, bf16[1024,1024]{1,0:T(8,128)(2,1)S(1)}, bf16[1024,1024]{1,0:T(8,128)(2,1)}) custom-call(bf16[512,1024]{1,0:T(8,128)(2,1)S(1)} %bitcast.8, bf16[1024,1024]{1,0:T(8,128)(2,1)} %metric_hbm.1), custom_call_target="tpu_custom_call" | custom-call | flops 8589934592 | bytes 4194304 | tf_op jit(solution)/shard_map/own/pallas_call | solution.py:292
  30.8 0.0 copy-start.1
  30.8 1.3 %copy-done.1 = bf16[1024,1024]{1,0:T(8,128)(2,1)} copy-done((bf16[1024,1024]{1,0:T(8,128)(2,1)}, bf16[1024,1024]{1,0:T(8,128)(2,1)S(1)}, u32[]{:S(2)}) %copy-start.1) | copy-done | bytes 2097176
  32.2 7.6 %all-to-all-done.1.mine_ref = bf16[16,4,8,1024]{3,2,1,0:T(8,128)(2,1)S(1)} async-done(((bf16[16,4,8,1024]{3,2,1,0:T(8,128)(2,1)}), bf16[16,4,8,1024]{3,2,1,0:T(8,128)(2,1)S(1)}, u32[]{:S(2)}, u32[]{:S(2)}) %all-to-all-start.1) | async-done | bytes 1048608 | tf_op jit(solution)/shard_map/all_to_all | solution.py:271
  39.7 3.5 %collective-permute-start = (bf16[16,4,8,1024]{3,2,1,0:T(8,128)(2,1)S(1)}, bf16[16,4,8,1024]{3,2,1,0:T(8,128)(2,1)S(1)}, u32[]{:S(2)}, u32[]{:S(2)}) collective-permute-start(bf16[16,4,8,1024]{3,2,1,0:T(8,128)(2,1)S(1)} %all-to-all-done.1.mine_ref), channel_id=1, source_target_pairs={{0,8},{8,0},{16,24},{24,16},{32,40},{40,32},{48,56},{56,48},{64,72... | collective-permute-start | bytes 3145736 | tf_op jit(solution)/shard_map/ppermute | solution.py:297
  43.3 2.3 %collective-permute-done.other_ref = bf16[16,4,8,1024]{3,2,1,0:T(8,128)(2,1)S(1)} collective-permute-done((bf16[16,4,8,1024]{3,2,1,0:T(8,128)(2,1)S(1)}, bf16[16,4,8,1024]{3,2,1,0:T(8,128)(2,1)S(1)}, u32[]{:S(2)}, u32[]{:S(2)}) %collective-permute-start) | collective-permute-done | bytes 1048608 | tf_op jit(solution)/shard_map/ppermute | solution.py:297
  45.6 18.3 %core.1 = bf16[8,512,128]{2,1,0:T(8,128)(2,1)S(1)} custom-call(s32[1]{0:T(128)} %bitcast.core_ref, bf16[16,4,8,1024]{3,2,1,0:T(8,128)(2,1)S(1)} %all-to-all-done.1.mine_ref, bf16[16,4,8,1024]{3,2,1,0:T(8,128)(2,1)S(1)} %collective-permute-done.other_ref, bf16[1024,1024]{1,0:T(8,128)(2,1)} %metric_hbm.1, ...), custom_call_target="tpu_custom_call" | custom-call | flops 17179869184 | bytes 4194304 | tf_op jit(solution)/shard_map/core/pallas_call | solution.py:299
  63.9 31.6 %all_to_all.16.got_ref = bf16[8,512,128]{2,1,0:T(8,128)(2,1)S(1)} all-to-all(bf16[8,512,128]{2,1,0:T(8,128)(2,1)S(1)} %core.1), channel_id=1, replica_groups=mesh['wide'=32,'narrow'=8] {'narrow'}, dimensions={0} | all-to-all | bytes 2097152 | tf_op jit(solution)/shard_map/all_to_all | solution.py:310
  95.5 2.6 %join.1 = f32[4096,128]{1,0:T(8,128)} custom-call(bf16[8,512,128]{2,1,0:T(8,128)(2,1)S(1)} %all_to_all.16.got_ref), custom_call_target="tpu_custom_call" | custom-call | flops 1073741824 | bytes 4194304 | tf_op jit(solution)/shard_map/join/pallas_call | solution.py:311
  (2 shorter events, 0.0 us)
Async XLA Ops:
  0.0 24.8 %copy-start = (bf16[512,1,1024]{2,0,1:T(8,128)(2,1)S(1)}, bf16[512,1,1024]{2,0,1:T(8,128)(2,1)}, u32[]{:S(2)}) copy-start(bf16[512,1,1024]{2,0,1:T(8,128)(2,1)} %param.2) | copy-start | bytes 3145732
  18.0 21.7 %all-to-all-start.1 = ((bf16[16,4,8,1024]{3,2,1,0:T(8,128)(2,1)}), bf16[16,4,8,1024]{3,2,1,0:T(8,128)(2,1)S(1)}, u32[]{:S(2)}, u32[]{:S(2)}) async-start(bf16[16,4,8,1024]{3,2,1,0:T(8,128)(2,1)} %broadcast_in_dim.16), calls=%async_computation.1 | async-start | bytes 2097152 | tf_op jit(solution)/shard_map/all_to_all | solution.py:271
  30.8 1.3 %copy-start.1 = (bf16[1024,1024]{1,0:T(8,128)(2,1)}, bf16[1024,1024]{1,0:T(8,128)(2,1)S(1)}, u32[]{:S(2)}) copy-start(bf16[1024,1024]{1,0:T(8,128)(2,1)S(1)} %get-tuple-element.13.spread_hbm) | copy-start | bytes 6291460
  39.7 5.8 %collective-permute-start = (bf16[16,4,8,1024]{3,2,1,0:T(8,128)(2,1)S(1)}, bf16[16,4,8,1024]{3,2,1,0:T(8,128)(2,1)S(1)}, u32[]{:S(2)}, u32[]{:S(2)}) collective-permute-start(bf16[16,4,8,1024]{3,2,1,0:T(8,128)(2,1)S(1)} %all-to-all-done.1.mine_ref), channel_id=1, source_target_pairs={{0,8},{8,0},{16,24},{24,16},{32,40},{40,32},{48,56},{56,48},{64,72... | collective-permute-start | bytes 3145736 | tf_op jit(solution)/shard_map/ppermute | solution.py:297

commit v5 on v4

--- a/solution.py
+++ b/solution.py
@@ -126,31 +126,21 @@
     out_ref[half:, :half] = -fmm(out_ref[half:, half:], fmm(lower, top))
 
 
-def own_kernel(rows_ref, metric_ref, proj_ref, spread_ref, spread_t_ref):
+def own_kernel(rows_ref, metric_ref, proj_ref, spread_ref):
     proj_ref[...] = mm(rows_ref[...], metric_ref[...]).astype(BF16)
-    for ref, cols in ((spread_ref, 256), (spread_t_ref, 512)):
-        per = cols // 8
-        r = lax.broadcasted_iota(jnp.int32, (1024, 1024), 0)
-        c = lax.broadcasted_iota(jnp.int32, (1024, 1024), 1)
-        dst, lane = c // 128, c % 128
-        want = (lane // per) * cols + (lane % per) * 8 + dst
-        ref[...] = jnp.where(r == want, 1.0, 0.0).astype(BF16)
-
-
-def packed(values, groups, spread):
-    size = values.shape[0] // groups
-    side = jnp.concatenate([values[g * size : (g + 1) * size] for g in range(groups)], axis=1)
-    return mm(side.astype(BF16), spread).astype(BF16)
+    r = lax.broadcasted_iota(jnp.int32, (1024, 1024), 0)
+    c = lax.broadcasted_iota(jnp.int32, (1024, 1024), 1)
+    spread_ref[...] = jnp.where(r == (c % 128) * 8 + c // 128, 1.0, 0.0).astype(BF16)
 
 
 def core_kernel(
-    core_ref, mine_ref, other_ref, metric_hbm, own_proj_hbm, spread_hbm, spread_t_hbm, send_ref,
-    panel_ref, metric_ref, own_proj_ref, spread_ref, spread_t_ref, proj_ref, head_ref, own_ref,
+    core_ref, mine_ref, other_ref, metric_hbm, own_proj_hbm, spread_hbm, send_ref,
+    panel_ref, metric_ref, own_proj_ref, spread_ref, proj_ref, head_ref, own_ref,
     own1_ref, upper_ref, upper1_ref, col_ref, inv0_ref, inv1_ref, sems,
 ):
     pairs = (
         (metric_hbm, metric_ref), (own_proj_hbm, own_proj_ref),
-        (spread_hbm, spread_ref), (spread_t_hbm, spread_t_ref),
+        (spread_hbm, spread_ref),
     )
     copies = [pltpu.make_async_copy(x, y, sems.at[i]) for i, (x, y) in enumerate(pairs)]
     for copy in copies:
@@ -184,7 +174,6 @@
     jobs += [slab(head_ref, proj_ref, r, c) for r in (0, PB) for c in range(0, 1024, PB) if r + c]
     factor_block(0.5 * (diag + diag.T), inv0_ref, jobs)
     copies[2].wait()
-    copies[3].wait()
 
     inv0 = inv0_ref[...]
     upper_ref[:, :PB] = fmm(inv0, head_ref[:PB, PB : 2 * PB])
@@ -220,9 +209,9 @@
         return job
 
     def finished():
-        strips = packed(col_ref[...], 4, spread_ref[...])
+        strips = mm(col_ref[...].astype(BF16), spread_ref[:PB]).astype(BF16)
         for s in range(8):
-            send_ref[s, :128] = strips[:, 128 * s : 128 * s + 128]
+            send_ref[s] = strips[:, 128 * s : 128 * s + 128]
 
     jobs = [column(0), column(PB), top(PB), top(2 * PB), under(PB), under(2 * PB)]
     jobs += [rest(r, c) for c in range(0, 768, PB) for r in (0, PB)] + [finished]
@@ -231,26 +220,15 @@
     inv = inv1_ref[...]
     col = fmm_nt(own1_ref[:, :PB], inv)
     upper = fmm(inv, upper1_ref[...])
-    trail = packed(own1_ref[:, PB:] - fmm(col, upper), 2, spread_t_ref[...])
-    strips = packed(col, 4, spread_ref[...])
+    trail = own1_ref[:, PB:] - fmm(col, upper)
+    strips = mm(jnp.concatenate([col.astype(BF16), trail.astype(BF16)], axis=1), spread_ref[PB:])
     for s in range(8):
-        send_ref[s, 128:256] = strips[:, 128 * s : 128 * s + 128]
-        send_ref[s, 256:] = trail[:, 128 * s : 128 * s + 128]
+        send_ref[s] = (strips[:, 128 * s : 128 * s + 128] + send_ref[s].astype(F32)).astype(BF16)
 
 
 def join_kernel(got_ref, out_ref):
-    group = pl.program_id(0)
-    lane = lax.broadcasted_iota(jnp.int32, (128, 128), 1)
-    parts = []
-    for s in range(8):
-        a, b = got_ref[s, :128].astype(F32), got_ref[s, 128:256].astype(F32)
-        t = got_ref[s, pl.ds(256 + 128 * (group % 2), 128)].astype(F32)
-        x = pltpu.roll(a, (128 - 32 * group) % 128, 1)
-        y = pltpu.roll(b, (160 - 32 * group) % 128, 1)
-        z = pltpu.roll(t, (192 - 64 * (group // 2)) % 128, 1)
-        parts.append(jnp.where(lane < 32, x, jnp.where(lane < 64, y, z)))
-    stacked = jnp.stack(parts, 0)
-    out_ref[...] = pltpu.einshape("skl->ksl", stacked).reshape(1024, 128)
+    stacked = got_ref[...].astype(F32)
+    out_ref[...] = pltpu.einshape("skl->ksl", stacked).reshape(out_ref.shape)
 
 
 def call(kernel, outs, flops, name, scratch=(), sems=(), **more):
@@ -289,8 +267,8 @@
         )
 
     column = spread_to(rows[:4], narrow, "narrow").transpose(1, 0, 2)
-    own_proj, spread, spread_t = call(
-        own_kernel, [((row_count, n), BF16), ((1024, 1024), BF16), ((1024, 1024), BF16)], 8 << 30, "own"
+    own_proj, spread = call(
+        own_kernel, [((row_count, n), BF16), ((1024, 1024), BF16)], 8 << 30, "own"
     )(rows, metric)
     mine = spread_to(column, plane, "wide", same_core)
     mine, own_proj = lax.optimization_barrier((mine, own_proj))
@@ -300,17 +278,17 @@
         core_kernel, [((8, row_count, 128), BF16)], 16 << 30, "core",
         [
             ((4 * PB, n), BF16), ((n, n), BF16), ((row_count, n), BF16), ((1024, 1024), BF16),
-            ((1024, 1024), BF16), ((2 * PB, n), BF16), ((2 * PB, 4 * PB), F32),
+            ((2 * PB, n), BF16), ((2 * PB, 4 * PB), F32),
             ((row_count, 4 * PB), F32), ((row_count, 3 * PB), F32), ((PB, 3 * PB), F32),
             ((PB, 2 * PB), F32), ((row_count, PB), F32), ((PB, PB), F32), ((PB, PB), F32),
         ],
-        [pltpu.SemaphoreType.DMA((4,))],
-        in_specs=[pl.BlockSpec(memory_space=pltpu.SMEM), vmem, vmem, hbm, hbm, hbm, hbm],
-    )(core.reshape(1), mine, other, metric, own_proj, spread, spread_t)
+        [pltpu.SemaphoreType.DMA((3,))],
+        in_specs=[pl.BlockSpec(memory_space=pltpu.SMEM), vmem, vmem, hbm, hbm, hbm],
+    )(core.reshape(1), mine, other, metric, own_proj, spread)
     got = lax.all_to_all(send, "narrow", 0, 0, tiled=True)
     out = call(
         join_kernel, [((row_count * 8, 128), F32)], 1 << 30, "join",
-        grid=(4,), in_specs=[pl.BlockSpec((8, 512, 128), lambda g: (0, 0, 0))],
+        grid=(4,), in_specs=[pl.BlockSpec((8, 128, 128), lambda g: (0, g, 0))],
         out_specs=pl.BlockSpec((1024, 128), lambda g: (g, 0)),
     )(got)
     return out.reshape(row_count, 8, 1, 128)

time: 98.3 us -> 97.7 us (level)
  Pallas kernels: 26.9 us -> 24 us
  waiting for transfers between devices: 9.84 us -> 12.1 us
    all_to_all x1, waiting for transfers between devices: 7.56 us -> 9.85 us  [spread_to(): lax.all_to_all(wide, axis, 0, 0, tiled=True, axis_index_groups=groups)]
    pallas_call x1, Pallas kernels: 6.05 us -> 3.77 us  [local(): call(own_kernel, [((row_count, n), BF16), ((1024, 1024), BF16)], 8 << 30,...]
  transfers between devices with their start and end apart: 2 -> 2, of which waited for: 2 -> 2; matrix products, arithmetic and copies ran while one was open for 0% -> 0% of each run, Pallas kernels for 6% -> 4%
where the time goes in v5:
time: 97.7 us; the launch traced here: 97.4 us
  blocking collectives  47.6 us (49%)
  Pallas kernels  24 us (25%)
  waiting for transfers between devices  12.1 us (12%)
  starting transfers between devices  10.3 us (11%)
  local copies, waits for them, and re-layouts  3.28 us (3%)
    all_to_all x1, blocking collectives, local(): got = lax.all_to_all(send, 'narrow', 0, 0, tiled=True)  31.6 us
    pallas_call x1, Pallas kernels, local(): call(core_kernel, [((8, row_count, 128), BF16)], 16 << 30, 'core', [((4 *...  18.2 us
    all_to_all x1, blocking collectives, spread_to(): lax.all_to_all(wide, axis, 0, 0, tiled=True, axis_index_groups=groups)  16 us
    all_to_all x1, waiting for transfers between devices, spread_to(): lax.all_to_all(wide, axis, 0, 0, tiled=True, axis_index_groups=groups)  9.85 us
    all_to_all x1, starting transfers between devices, spread_to(): lax.all_to_all(wide, axis, 0, 0, tiled=True, axis_index_groups=groups)  6.75 us
    pallas_call x1, Pallas kernels, local(): call(own_kernel, [((row_count, n), BF16), ((1024, 1024), BF16)], 8 << 30,...  3.77 us
    ppermute x1, starting transfers between devices, local(): other = lax.ppermute(mine, 'wide', swap)  3.55 us
    ppermute x1, waiting for transfers between devices, local(): other = lax.ppermute(mine, 'wide', swap)  2.29 us
  transfers between devices with their start and end apart: 2, of which 2 were waited for; matrix products, arithmetic and copies ran while one was open for 0% of the time, Pallas kernels for 4%

profile of v5, /device:TPU:1, one launch (start us, length us, event | category | flops | bytes accessed | tf_op | source)
XLA Modules:
  0.0 97.4 jit_solution(9280267063269824884)
XLA Ops:
  0.0 0.0 copy-start
  0.0 0.8 slice_bitcast_fusion
  0.8 16.0 %all_to_all.15 = bf16[8,4,1024]{2,1,0:T(4,128)(2,1)S(1)} all-to-all(bf16[8,4,1024]{2,1,0:T(4,128)(2,1)S(1)} %broadcast_in_dim.7), channel_id=1, replica_groups=mesh['wide'=32,'narrow'=8] {'narrow'}, dimensions={0} | all-to-all | bytes 131072 | tf_op jit(solution)/shard_map/all_to_all | solution.py:249
  16.9 1.1 %broadcast_in_dim.16 = bf16[16,4,8,1024]{3,2,1,0:T(8,128)(2,1)} broadcast(bf16[4,8,1024]{2,1,0:T(8,128)(2,1)S(1)} %copy.4), dimensions={1,2,3} | broadcast | bytes 1114112 | tf_op jit(solution)/shard_map/broadcast_in_dim | solution.py:248
  18.0 6.8 %all-to-all-start.1 = ((bf16[16,4,8,1024]{3,2,1,0:T(8,128)(2,1)}), bf16[16,4,8,1024]{3,2,1,0:T(8,128)(2,1)S(1)}, u32[]{:S(2)}, u32[]{:S(2)}) async-start(bf16[16,4,8,1024]{3,2,1,0:T(8,128)(2,1)} %broadcast_in_dim.16), calls=%async_computation.1 | async-start | bytes 2097152 | tf_op jit(solution)/shard_map/all_to_all | solution.py:249
  24.8 0.0 copy-done
  24.8 3.8 %own.1 = (bf16[512,1024]{1,0:T(8,128)(2,1)S(1)}, bf16[1024,1024]{1,0:T(8,128)(2,1)S(1)}) custom-call(bf16[512,1024]{1,0:T(8,128)(2,1)S(1)} %bitcast.8, bf16[1024,1024]{1,0:T(8,128)(2,1)} %metric_hbm.1), custom_call_target="tpu_custom_call" | custom-call | flops 8589934592 | bytes 4194304 | tf_op jit(solution)/shard_map/own/pallas_call | solution.py:270
  28.5 0.0 copy-start.1
  28.6 1.3 %copy-done.1 = bf16[1024,1024]{1,0:T(8,128)(2,1)} copy-done((bf16[1024,1024]{1,0:T(8,128)(2,1)}, bf16[1024,1024]{1,0:T(8,128)(2,1)S(1)}, u32[]{:S(2)}) %copy-start.1) | copy-done | bytes 2097176
  29.9 9.8 %all-to-all-done.1.mine_ref = bf16[16,4,8,1024]{3,2,1,0:T(8,128)(2,1)S(1)} async-done(((bf16[16,4,8,1024]{3,2,1,0:T(8,128)(2,1)}), bf16[16,4,8,1024]{3,2,1,0:T(8,128)(2,1)S(1)}, u32[]{:S(2)}, u32[]{:S(2)}) %all-to-all-start.1) | async-done | bytes 1048608 | tf_op jit(solution)/shard_map/all_to_all | solution.py:249
  39.7 3.5 %collective-permute-start = (bf16[16,4,8,1024]{3,2,1,0:T(8,128)(2,1)S(1)}, bf16[16,4,8,1024]{3,2,1,0:T(8,128)(2,1)S(1)}, u32[]{:S(2)}, u32[]{:S(2)}) collective-permute-start(bf16[16,4,8,1024]{3,2,1,0:T(8,128)(2,1)S(1)} %all-to-all-done.1.mine_ref), channel_id=1, source_target_pairs={{0,8},{8,0},{16,24},{24,16},{32,40},{40,32},{48,56},{56,48},{64,72... | collective-permute-start | bytes 3145736 | tf_op jit(solution)/shard_map/ppermute | solution.py:275
  43.3 2.3 %collective-permute-done.other_ref = bf16[16,4,8,1024]{3,2,1,0:T(8,128)(2,1)S(1)} collective-permute-done((bf16[16,4,8,1024]{3,2,1,0:T(8,128)(2,1)S(1)}, bf16[16,4,8,1024]{3,2,1,0:T(8,128)(2,1)S(1)}, u32[]{:S(2)}, u32[]{:S(2)}) %collective-permute-start) | collective-permute-done | bytes 1048608 | tf_op jit(solution)/shard_map/ppermute | solution.py:275
  45.6 18.2 %core.1 = bf16[8,512,128]{2,1,0:T(8,128)(2,1)S(1)} custom-call(s32[1]{0:T(128)} %bitcast.core_ref, bf16[16,4,8,1024]{3,2,1,0:T(8,128)(2,1)S(1)} %all-to-all-done.1.mine_ref, bf16[16,4,8,1024]{3,2,1,0:T(8,128)(2,1)S(1)} %collective-permute-done.other_ref, bf16[1024,1024]{1,0:T(8,128)(2,1)} %metric_hbm.1, ...), custom_call_target="tpu_custom_call" | custom-call | flops 17179869184 | bytes 4194304 | tf_op jit(solution)/shard_map/core/pallas_call | solution.py:277
  63.8 31.6 %all_to_all.16.got_ref = bf16[8,512,128]{2,1,0:T(8,128)(2,1)S(1)} all-to-all(bf16[8,512,128]{2,1,0:T(8,128)(2,1)S(1)} %core.1), channel_id=1, replica_groups=mesh['wide'=32,'narrow'=8] {'narrow'}, dimensions={0} | all-to-all | bytes 2097152 | tf_op jit(solution)/shard_map/all_to_all | solution.py:288
  95.4 2.0 %join.1 = f32[4096,128]{1,0:T(8,128)} custom-call(bf16[8,512,128]{2,1,0:T(8,128)(2,1)S(1)} %all_to_all.16.got_ref), custom_call_target="tpu_custom_call" | custom-call | flops 1073741824 | bytes 4194304 | tf_op jit(solution)/shard_map/join/pallas_call | solution.py:289
  (2 shorter events, 0.0 us)
Async XLA Ops:
  0.0 24.8 %copy-start = (bf16[512,1,1024]{2,0,1:T(8,128)(2,1)S(1)}, bf16[512,1,1024]{2,0,1:T(8,128)(2,1)}, u32[]{:S(2)}) copy-start(bf16[512,1,1024]{2,0,1:T(8,128)(2,1)} %param.2) | copy-start | bytes 3145732
  18.0 21.7 %all-to-all-start.1 = ((bf16[16,4,8,1024]{3,2,1,0:T(8,128)(2,1)}), bf16[16,4,8,1024]{3,2,1,0:T(8,128)(2,1)S(1)}, u32[]{:S(2)}, u32[]{:S(2)}) async-start(bf16[16,4,8,1024]{3,2,1,0:T(8,128)(2,1)} %broadcast_in_dim.16), calls=%async_computation.1 | async-start | bytes 2097152 | tf_op jit(solution)/shard_map/all_to_all | solution.py:249
  28.5 1.3 %copy-start.1 = (bf16[1024,1024]{1,0:T(8,128)(2,1)}, bf16[1024,1024]{1,0:T(8,128)(2,1)S(1)}, u32[]{:S(2)}) copy-start(bf16[1024,1024]{1,0:T(8,128)(2,1)S(1)} %get-tuple-element.12.spread_hbm) | copy-start | bytes 6291460
  39.7 5.8 %collective-permute-start = (bf16[16,4,8,1024]{3,2,1,0:T(8,128)(2,1)S(1)}, bf16[16,4,8,1024]{3,2,1,0:T(8,128)(2,1)S(1)}, u32[]{:S(2)}, u32[]{:S(2)}) collective-permute-start(bf16[16,4,8,1024]{3,2,1,0:T(8,128)(2,1)S(1)} %all-to-all-done.1.mine_ref), channel_id=1, source_target_pairs={{0,8},{8,0},{16,24},{24,16},{32,40},{40,32},{48,56},{56,48},{64,72... | collective-permute-start | bytes 3145736 | tf_op jit(solution)/shard_map/ppermute | solution.py:275
